TPU v7x, 256 devices: a whole 4x4x8 slice. The times are simulated.
256 devices in a mesh: ctx: 32 (over y, x, core), ep: 8 (over z).
Axes of the slice: x: 4, y: 4, z: 8, core: 2. Of those that a mesh axis runs over, the one named last changes fastest.
Arguments:
- out_grad: bfloat16 [8192, 2048], P('ctx'), may hold values from -12 to 12
- gate_values: bfloat16 [8192, 8], P('ctx'), may hold values from 0.049804688 to 0.3984375
- expert_ids: int32 [8192, 8], P('ctx'), may hold values from 0 to 63, all different within a row; in each aligned block of 256 rows (0 to 255, 256 to 511, ...) at most 48 rows name the same one
- segment_ids: int32 [8192], P('ctx'), may hold values from 0 to 15, never falling along the last dimension, each value on 1 to 1793 neighbouring positions
- gate_pre: bfloat16 [256, 32, 48, 256], P(('ctx', 'ep')), may hold values from -6 to 6
- up_pre: bfloat16 [256, 32, 48, 256], P(('ctx', 'ep')), may hold values from -6 to 6
- w_gate: bfloat16 [256, 2048, 256], P(('ctx', 'ep')), may hold values from -0.125 to 0.125
- w_up: bfloat16 [256, 2048, 256], P(('ctx', 'ep')), may hold values from -0.125 to 0.125
- w_down: bfloat16 [256, 256, 2048], P(('ctx', 'ep')), may hold values from -0.1875 to 0.1875
- queries: bfloat16 [8192, 2048], P('ctx', 'ep'), may hold values from -0.015625 to 0.015625
- keys: bfloat16 [8192, 2048], P('ctx', 'ep'), may hold values from -0.015625 to 0.015625
- values: bfloat16 [8192, 2048], P('ctx', 'ep'), may hold values from -6 to 6
Outputs:
- query_grad: bfloat16 [8192, 2048], P('ctx', 'ep')
- key_grad: bfloat16 [8192, 2048], P('ctx', 'ep')
- value_grad: bfloat16 [8192, 2048], P('ctx', 'ep')
- down_grad: float32 [256, 256, 2048], P(('ctx', 'ep'))
Inputs may be any that keep to these rules, and one draw needn't show every extreme that they name: `expert_ids`: each token names 8 different experts. Among the 256 tokens of one context shard at most 48 name the same expert, and in every draw some shard has exactly 48 tokens that name one expert. `segment_ids`: document numbers never fall along the tokens; a document has 1 to 1793 tokens and one has exactly 1793, so that no document covers more than eight context shards of 256 tokens.
All inputs are finite; a program needn't handle non-finite values.
Results may differ from a plain program's by a relative error of at most 0.008.
Values may be sent and summed in bfloat16 or wider, within the bound.
A program may use at most 128 MiB of HBM per device.

v0:
```python
import jax
import jax.numpy as jnp
from jax import lax
from jax.sharding import PartitionSpec as P

HEAD_DIM = 128


HIGHEST = lax.Precision.HIGHEST


def prefix(shard, axis, join, neutral, backward):
    count = lax.axis_size(axis)
    place = lax.axis_index(axis)
    ahead = count - 1 - place if backward else place
    gathered = jax.tree.map(
        lambda a, kind: lax.all_gather(a.astype(kind), axis),
        shard,
        jax.tree.map(lambda a: jnp.bfloat16 if a.dtype == jnp.float32 else a.dtype, shard),
    )
    state = jax.tree.map(lambda a, e: jnp.zeros_like(a) + jnp.asarray(e, a.dtype), shard, neutral)

    def one(hop, state):
        source = count - 1 - hop if backward else hop
        return join(
            state,
            jax.tree.map(
                lambda a, own: lax.dynamic_index_in_dim(a, source, 0, False).astype(own.dtype),
                gathered,
                shard,
            ),
        )

    return lax.fori_loop(0, ahead, one, state)


def count_before(flat_ids, expert_count):
    labels = jnp.arange(expert_count, dtype=jnp.int32)
    onehot = (flat_ids[:, None] == labels[None, :]).astype(jnp.int32)
    before = jnp.cumsum(onehot, axis=0) - onehot
    return jnp.sum(before * onehot, axis=1)


def expert_rows(cotangent, pre_gate, pre_up, gate_matrix, up_matrix, down_matrix):
    down_part = lax.dot_general(
        cotangent, down_matrix, (((1,), (1,)), ((), ())), preferred_element_type=jnp.float32
    )
    gate_value = pre_gate.astype(jnp.float32)
    up_value = pre_up.astype(jnp.float32)
    sigmoid_gate = jax.nn.sigmoid(gate_value)
    hidden = (gate_value * sigmoid_gate * up_value).astype(jnp.bfloat16)
    down_grad = lax.dot_general(
        hidden, cotangent, (((0,), (0,)), ((), ())), preferred_element_type=jnp.float32
    )
    gate_delta = (
        down_part * up_value * sigmoid_gate * (1.0 + gate_value * (1.0 - sigmoid_gate))
    ).astype(jnp.bfloat16)
    up_delta = (down_part * gate_value * sigmoid_gate).astype(jnp.bfloat16)
    input_part = lax.dot_general(
        gate_delta, gate_matrix, (((1,), (1,)), ((), ())), preferred_element_type=jnp.float32
    )
    input_part = input_part + lax.dot_general(
        up_delta, up_matrix, (((1,), (1,)), ((), ())), preferred_element_type=jnp.float32
    )
    return (input_part.astype(jnp.bfloat16), down_grad)


def gather_back(returned, owner_of, slot_rank, is_mine, offset, piece_slots, tok_rows, top_count):
    model_width = returned.shape[2]
    local_rank = slot_rank - offset
    usable = is_mine & (local_rank >= 0) & (local_rank < piece_slots)
    row_index = jnp.where(usable, owner_of * piece_slots + local_rank, 0)
    picked = jnp.take(returned.reshape(-1, model_width), row_index, axis=0).astype(jnp.float32)
    picked = picked * usable.astype(jnp.float32)[:, None]
    return jnp.sum(picked.reshape(tok_rows, top_count, model_width), axis=1)


def join_states(earlier, latter):
    state_a, doc_a, whole_a, filled_a = earlier
    state_b, doc_b, whole_b, filled_b = latter
    empty_a = filled_a == 0.0
    empty_b = filled_b == 0.0
    same_doc = doc_a == doc_b
    carried = empty_b | (whole_b > 0.0) & same_doc
    state_sum = state_b + jnp.where(carried[..., None, None, None], state_a, 0.0)
    doc_id = jnp.where(empty_b, doc_a, doc_b)
    joined = jnp.where((whole_a > 0.0) & (whole_b > 0.0) & same_doc, 1.0, 0.0)
    whole_doc = jnp.where(empty_b, whole_a, jnp.where(empty_a, whole_b, joined))
    return (state_sum, doc_id, whole_doc, jnp.maximum(filled_a, filled_b))


def within_block(query3, key3, value3, cot3, segment):
    positions = jnp.arange(segment.shape[0], dtype=jnp.int32)
    allowed = (
        (positions[:, None] >= positions[None, :]) & (segment[:, None] == segment[None, :])
    ).astype(jnp.float32)
    cot_value = (
        jnp.einsum("the,she->hts", cot3, value3, preferred_element_type=jnp.float32) * allowed[None]
    )
    query_key = (
        jnp.einsum("the,she->hts", query3, key3, preferred_element_type=jnp.float32) * allowed[None]
    )
    query_grad = jnp.einsum("hts,she->the", cot_value, key3.astype(jnp.float32), precision=HIGHEST)
    key_grad = jnp.einsum("hts,the->she", cot_value, query3.astype(jnp.float32), precision=HIGHEST)
    value_grad = jnp.einsum("hts,the->she", query_key, cot3.astype(jnp.float32), precision=HIGHEST)
    return (query_grad, key_grad, value_grad)


def end_states(query3, key3, value3, cot3, segment):
    last_mask = (segment == segment[-1])[:, None, None]
    first_mask = (segment == segment[0])[:, None, None]
    forward_state = jnp.einsum(
        "the,thf->hef",
        jnp.where(last_mask, key3, jnp.zeros_like(key3)),
        value3,
        preferred_element_type=jnp.float32,
    )
    backward_state = jnp.einsum(
        "the,thf->hef",
        jnp.where(first_mask, query3, jnp.zeros_like(query3)),
        cot3,
        preferred_element_type=jnp.float32,
    )
    return (forward_state, backward_state)


def across_blocks(key3, value3, cot3, before_mask, after_mask, state_in, back_in):
    query_part = (
        jnp.einsum("thf,hef->the", cot3.astype(jnp.float32), state_in, precision=HIGHEST)
        * before_mask
    )
    key_part = (
        jnp.einsum("thf,hef->the", value3.astype(jnp.float32), back_in, precision=HIGHEST)
        * after_mask
    )
    value_part = (
        jnp.einsum("the,hef->thf", key3.astype(jnp.float32), back_in, precision=HIGHEST)
        * after_mask
    )
    return (query_part, key_part, value_part)


def local(
    out_grad,
    gate_values,
    expert_ids,
    segment_ids,
    gate_pre,
    up_pre,
    w_gate,
    w_up,
    w_down,
    queries,
    keys,
    values,
):
    owners = lax.axis_size("ctx")
    groups = lax.axis_size("ep")
    part_count = groups // 2
    device_place = lax.axis_index("ep")
    parity = device_place // part_count
    tok_rows, model_width = out_grad.shape
    top_count = expert_ids.shape[1]
    slot_count = gate_pre.shape[2]
    flat_ids = expert_ids.reshape(-1)
    slot_rank = count_before(flat_ids, 2 * owners)
    owner_of = flat_ids // 2
    is_mine = flat_ids % 2 == parity
    token_of = jnp.arange(tok_rows * top_count, dtype=jnp.int32) // top_count
    dump_slot = owners * slot_count
    position = jnp.where(is_mine, owner_of * slot_count + slot_rank, dump_slot)
    slot_token = jnp.full((dump_slot,), tok_rows, jnp.int32).at[position].set(token_of, mode="drop")
    slot_gate = (
        jnp.zeros((dump_slot,), gate_values.dtype)
        .at[position]
        .set(gate_values.reshape(-1), mode="drop")
    )
    padded = jnp.concatenate([out_grad, jnp.zeros((1, model_width), out_grad.dtype)], axis=0)
    send_rows = jnp.take(padded, slot_token, axis=0).reshape(owners, slot_count, model_width)
    send_gates = slot_gate.reshape(owners, slot_count)
    pre_gate = gate_pre[0].reshape(dump_slot, -1)
    pre_up = up_pre[0].reshape(dump_slot, -1)
    got_rows, got_gates = (
        lax.all_to_all(send_rows, "ctx", split_axis=0, concat_axis=0, tiled=True),
        lax.all_to_all(send_gates, "ctx", split_axis=0, concat_axis=0, tiled=True),
    )
    cotangent = (got_gates[..., None].astype(jnp.float32) * got_rows.astype(jnp.float32)).astype(
        jnp.bfloat16
    )
    input_part, down_grad = expert_rows(
        cotangent.reshape(dump_slot, model_width), pre_gate, pre_up, w_gate[0], w_up[0], w_down[0]
    )
    returned = lax.all_to_all(
        input_part.reshape(owners, slot_count, model_width),
        "ctx",
        split_axis=0,
        concat_axis=0,
        tiled=True,
    )
    offset = 0
    token_sum = gather_back(
        returned, owner_of, slot_rank, is_mine, offset, slot_count, tok_rows, top_count
    )
    head_sum = lax.psum_scatter(token_sum, "ep", scatter_dimension=1, tiled=True)
    head_cot = head_sum.astype(jnp.bfloat16)
    heads_here = queries.shape[1] // HEAD_DIM
    head_shape = (tok_rows, heads_here, HEAD_DIM)
    query3 = queries.reshape(head_shape)
    key3 = keys.reshape(head_shape)
    value3 = values.reshape(head_shape)
    cot3 = head_cot.reshape(head_shape)
    inner_query, inner_key, inner_value = within_block(query3, key3, value3, cot3, segment_ids)
    forward_state, backward_state = end_states(query3, key3, value3, cot3, segment_ids)
    seg_float = segment_ids.astype(jnp.float32)
    whole_doc = (segment_ids[0] == segment_ids[-1]).astype(jnp.float32)
    filled = jnp.ones((), jnp.float32)
    forward_element = (forward_state, seg_float[-1], whole_doc, filled)
    backward_element = (backward_state, seg_float[0], whole_doc, filled)
    identity = (
        jnp.zeros_like(forward_state),
        jnp.full((), -1.0, jnp.float32),
        jnp.ones((), jnp.float32),
        jnp.zeros((), jnp.float32),
    )
    before = prefix(forward_element, "ctx", join_states, identity, False)
    following = prefix(backward_element, "ctx", join_states, identity, True)
    before_mask = (seg_float == before[1]).astype(jnp.float32)[:, None, None]
    after_mask = (seg_float == following[1]).astype(jnp.float32)[:, None, None]
    outer_query, outer_key, outer_value = across_blocks(
        key3, value3, cot3, before_mask, after_mask, before[0], following[0]
    )
    query_grad = (inner_query + outer_query).astype(jnp.bfloat16).reshape(tok_rows, -1)
    key_grad = (inner_key + outer_key).astype(jnp.bfloat16).reshape(tok_rows, -1)
    value_grad = (inner_value + outer_value).astype(jnp.bfloat16).reshape(tok_rows, -1)
    return (query_grad, key_grad, value_grad, down_grad[None])


def solution(mesh):
    return jax.shard_map(
        local,
        mesh=mesh,
        in_specs=(
            P("ctx", None),
            P("ctx", None),
            P("ctx", None),
            P("ctx"),
            P(("ctx", "ep"), None, None, None),
            P(("ctx", "ep"), None, None, None),
            P(("ctx", "ep"), None, None),
            P(("ctx", "ep"), None, None),
            P(("ctx", "ep"), None, None),
            P("ctx", "ep"),
            P("ctx", "ep"),
            P("ctx", "ep"),
        ),
        out_specs=(P("ctx", "ep"), P("ctx", "ep"), P("ctx", "ep"), P(("ctx", "ep"), None, None)),
        check_vma=False,
    )
```

profile of v0, /device:TPU:1, one launch (start us, length us, event | category | flops | bytes accessed | tf_op | source)
XLA Modules:
  0.0 583.6 jit_solution(10885707942131973153)
XLA Ops:
  8.0 1.0 copy.86
  9.4 0.8 copy.95
  10.3 18.1 %reduce-window.6 = s32[64,16,128]{2,1,0:T(8,128)S(1)} reduce-window(s32[64,16,128]{2,1,0:T(8,128)S(1)} %fusion.30, s32[]{:T(128)} %constant.168.clone.1), window={size=1x1x128 pad=0_0x0_0x127_0}, to_apply=%region_0.1 | reduce-window | flops 16646144 | bytes 1048580 | tf_op jit(solution)/shard_map/reduce-window
  29.9 14.6 %scatter_custom_fusion = bf16[1536]{0:T(1024)(128)(2,1)S(1)} fusion(s32[2048]{0:T(1024)S(1)} %bitcast.202, bf16[2048]{0:T(1024)(128)(2,1)S(1)} %reshape.395, bf16[]{:T(256)} %constant.177.clone.1), kind=kCustom, calls=%fused_computation.116 | custom fusion | bytes 3074 | tf_op jit(solution)/shard_map/scatter | solution.py:176
  45.2 8.6 %all-to-all-start = ((bf16[32,1,48]{2,1,0:T(2,128)(2,1)}), bf16[32,1,48]{2,1,0:T(2,128)(2,1)S(1)}, u32[]{:S(2)}, u32[]{:S(2)}) async-start(bf16[32,1,48]{2,1,0:T(2,128)(2,1)} %all_to_all.16), calls=%async_computation | async-start | bytes 32768 | tf_op jit(solution)/shard_map/all_to_all | solution.py:185
  53.8 8.0 %scatter_custom_fusion.1 = s32[1536]{0:T(1024)S(1)} fusion(s32[2048]{0:T(1024)S(1)} %bitcast.203, s32[2048]{0:T(1024)S(1)} %add_select_fusion.2, s32[]{:T(128)} %constant.178.clone.1), kind=kCustom, calls=%fused_computation.114 | custom fusion | bytes 6148 | tf_op jit(solution)/shard_map/scatter | solution.py:172
  62.1 7.1 %gather_fusion = bf16[1536,2048]{1,0:T(8,128)(2,1)} fusion(bf16[257,2048]{1,0:T(8,128)(2,1)S(1)} %concatenate.3, s32[2048]{0:T(1024)S(1)} %pad_clamp_fusion), kind=kCustom, calls=%fused_computation | custom fusion | bytes 12589056 | tf_op jit(solution)/shard_map/jit(_take)/gather | solution.py:179
  69.2 6.1 %broadcast_select_fusion = bf16[32,48,2048]{2,1,0:T(8,128)(2,1)} fusion(bf16[32,48,2048]{2,1,0:T(8,128)(2,1)} %bitcast.178, pred[32,48]{1,0:T(8,128)(4,1)S(1)} %broadcast_in_dim.109), kind=kLoop, calls=%fused_computation.10 | loop fusion | flops 3145728 | bytes 12584448 | tf_op jit(solution)/shard_map/jit(_take)/select_n | solution.py:179
  75.3 7.4 %all-to-all-start.1 = ((bf16[32,48,2048]{2,1,0:T(8,128)(2,1)}), bf16[32,48,2048]{2,1,0:T(8,128)(2,1)}, u32[]{:S(2)}, u32[]{:S(2)}) async-start(bf16[32,48,2048]{2,1,0:T(8,128)(2,1)} %broadcast_select_fusion), calls=%async_computation.1 | async-start | bytes 12582912 | tf_op jit(solution)/shard_map/all_to_all | solution.py:184
  82.8 72.9 %all-to-all-done.1 = bf16[32,48,2048]{2,1,0:T(8,128)(2,1)} async-done(((bf16[32,48,2048]{2,1,0:T(8,128)(2,1)}), bf16[32,48,2048]{2,1,0:T(8,128)(2,1)}, u32[]{:S(2)}, u32[]{:S(2)}) %all-to-all-start.1) | async-done | bytes 6291488 | tf_op jit(solution)/shard_map/all_to_all | solution.py:184
  155.7 4.0 multiply_convert_fusion
  159.8 2.5 fusion.11
  162.5 1.8 fusion.23
  164.3 4.5 add_convert_fusion
  168.8 9.7 %all-to-all-start.2 = ((bf16[32,48,2048]{2,1,0:T(8,128)(2,1)}), bf16[32,48,2048]{2,1,0:T(8,128)(2,1)}, u32[]{:S(2)}, u32[]{:S(2)}) async-start(bf16[32,48,2048]{2,1,0:T(8,128)(2,1)} %bitcast.177), calls=%async_computation.2 | async-start | bytes 12582912 | tf_op jit(solution)/shard_map/all_to_all | solution.py:193
  178.9 72.6 %all-to-all-done.2 = bf16[32,48,2048]{2,1,0:T(8,128)(2,1)} async-done(((bf16[32,48,2048]{2,1,0:T(8,128)(2,1)}), bf16[32,48,2048]{2,1,0:T(8,128)(2,1)}, u32[]{:S(2)}, u32[]{:S(2)}) %all-to-all-start.2) | async-done | bytes 6291488 | tf_op jit(solution)/shard_map/all_to_all | solution.py:193
  251.6 20.0 %gather_fusion.1 = bf16[2048,2048]{1,0:T(8,128)(2,1)} fusion(bf16[1536,2048]{1,0:T(8,128)(2,1)} %bitcast.24, s32[2048]{0:T(1024)S(1)} %broadcast_clamp_fusion), kind=kCustom, calls=%fused_computation.1 | custom fusion | bytes 16785408 | tf_op jit(solution)/shard_map/jit(_take)/gather | solution.py:73
  271.6 10.8 %multiply_reduce_fusion = f32[256,2048]{1,0:T(8,128)} fusion(bf16[2048,2048]{1,0:T(8,128)(2,1)} %gather_fusion.1, f32[256,8]{1,0:T(8,128)S(1)} %convert_element_type.196, pred[256,8]{1,0:T(8,128)(4,1)S(1)} %get-tuple-element.261), kind=kLoop, calls=%fused_computation.6 | loop fusion | flops 16252928 | bytes 10496000 | tf_op jit(solution)/shard_map/reduce_sum | solution.py:75
  283.4 1.3 broadcast_compare_fusion
  284.7 0.8 convolution_convert_fusion.1
  285.7 37.5 %reduce-scatter.2.cloned.1.call-done = f32[256,256]{1,0:T(8,128)} async-done(((f32[256,2048]{1,0:T(8,128)}), f32[256,256]{1,0:T(8,128)}) %reduce-scatter.2.cloned.1.call-update) | async-done | bytes 262160 | tf_op jit(solution)/shard_map/reduce_scatter | solution.py:204
  323.2 1.0 convert_element_type.197
  324.3 0.8 convolution_convert_fusion
  328.4 1.4 dynamic-update-slice.3
  329.8 1.4 dynamic-update-slice.2
  331.9 67.1 %all-reduce.5 = (bf16[32]{0:T(256)(128)(2,1)S(1)}, bf16[32]{0:T(256)(128)(2,1)S(1)}, bf16[32]{0:T(256)(128)(2,1)S(1)}, bf16[32]{0:T(256)(128)(2,1)S(1)}) all-reduce(bf16[32]{0:T(256)(128)(2,1)S(1)} %dynamic-update-slice, bf16[32]{0:T(256)(128)(2,1)S(1)} %dynamic-update-slice.1, ...), channel_id=1, replica_groups=mesh['ctx'=32,'ep'=8] {'ctx'}, use_global_device_ids=true, to_apply=%add.1 | all-reduce | flops 128 | bytes 512
  399.5 1.6 fusion.13
  401.2 5.3 while.32
  405.6 0.9 convert_add_fusion.4
  406.5 6.0 %convolution_bitcast_fusion = f32[1,256,2048]{2,1,0:T(8,128)} fusion(bf16[1536,256]{1,0:T(8,128)(2,1)S(1)} %bitcast.179, bf16[1536,2048]{1,0:T(8,128)(2,1)} %bitcast.176), kind=kOutput, calls=%fused_computation.11 | convolution fusion | flops 1610612736 | bytes 9175040 | tf_op jit(solution)/shard_map/dot_general | solution.py:52
  414.0 159.0 %while.33 = (s32[]{:T(128)}, f32[2,128,128]{2,1,0:T(8,128)S(1)}, f32[]{:T(128)}, s32[]{:T(128)}, bf16[32,2,128,128]{3,2,1,0:T(8,128)(2,1)}, /*index=5*/bf16[32]{...) while((s32[]{:T(128)}, f32[2,128,128]{2,1,0:T(8,128)S(1)}, ...), condition=%wide.region_10.11_spmd, body=%wide.region_9.10_spmd.sunk | while | flops 98316 | bytes 327934 | solution.py:34
  418.4 0.9 convert_add_fusion.5
  423.7 0.9 convert_add_fusion.5
  429.0 0.9 convert_add_fusion.5
  434.3 0.9 convert_add_fusion.5
  439.6 0.9 convert_add_fusion.5
  444.9 0.9 convert_add_fusion.5
  450.2 0.9 convert_add_fusion.5
  455.5 0.9 convert_add_fusion.5
  460.8 0.9 convert_add_fusion.5
  466.1 0.9 convert_add_fusion.5
  471.4 0.9 convert_add_fusion.5
  476.7 0.9 convert_add_fusion.5
  482.0 0.9 convert_add_fusion.5
  487.3 0.9 convert_add_fusion.5
  492.6 0.9 convert_add_fusion.5
  497.9 0.9 convert_add_fusion.5
  503.2 0.9 convert_add_fusion.5
  508.5 0.9 convert_add_fusion.5
  513.8 0.9 convert_add_fusion.5
  519.1 0.9 convert_add_fusion.5
  524.4 0.9 convert_add_fusion.5
  529.7 0.9 convert_add_fusion.5
  535.0 0.9 convert_add_fusion.5
  540.3 0.9 convert_add_fusion.5
  545.6 0.9 convert_add_fusion.5
  550.9 0.9 convert_add_fusion.5
  556.2 0.9 convert_add_fusion.5
  561.5 0.9 convert_add_fusion.5
  566.8 0.9 convert_add_fusion.5
  572.1 0.9 convert_add_fusion.5
  573.4 0.8 copy.114
  574.4 0.8 copy.113
  575.4 0.8 copy.112
  (179 shorter events, 64.9 us)
Async XLA Ops:
  8.0 154.5 %copy-start = (bf16[1,2048,256]{2,1,0:T(8,128)(2,1)S(1)}, bf16[1,2048,256]{2,1,0:T(8,128)(2,1)}, u32[]{:S(2)}) copy-start(bf16[1,2048,256]{2,1,0:T(8,128)(2,1)} %param.22) | copy-start | bytes 3145732
  8.0 54.0 %copy-start.4 = (bf16[256,2048]{1,0:T(8,128)(2,1)S(1)}, bf16[256,2048]{1,0:T(8,128)(2,1)}, u32[]{:S(2)}) copy-start(bf16[256,2048]{1,0:T(8,128)(2,1)} %param.16) | copy-start | bytes 3145732
  45.2 30.1 %all-to-all-start = ((bf16[32,1,48]{2,1,0:T(2,128)(2,1)}), bf16[32,1,48]{2,1,0:T(2,128)(2,1)S(1)}, u32[]{:S(2)}, u32[]{:S(2)}) async-start(bf16[32,1,48]{2,1,0:T(2,128)(2,1)} %all_to_all.16), calls=%async_computation | async-start | bytes 32768 | tf_op jit(solution)/shard_map/all_to_all | solution.py:185
  75.3 80.4 %all-to-all-start.1 = ((bf16[32,48,2048]{2,1,0:T(8,128)(2,1)}), bf16[32,48,2048]{2,1,0:T(8,128)(2,1)}, u32[]{:S(2)}, u32[]{:S(2)}) async-start(bf16[32,48,2048]{2,1,0:T(8,128)(2,1)} %broadcast_select_fusion), calls=%async_computation.1 | async-start | bytes 12582912 | tf_op jit(solution)/shard_map/all_to_all | solution.py:184
  155.7 4.0 copy-start.5
  155.7 4.0 copy-start.7
  155.7 4.1 copy-start.12
  159.8 2.7 copy-start.2
  162.5 1.8 copy-start.3
  168.8 82.8 %all-to-all-start.2 = ((bf16[32,48,2048]{2,1,0:T(8,128)(2,1)}), bf16[32,48,2048]{2,1,0:T(8,128)(2,1)}, u32[]{:S(2)}, u32[]{:S(2)}) async-start(bf16[32,48,2048]{2,1,0:T(8,128)(2,1)} %bitcast.177), calls=%async_computation.2 | async-start | bytes 12582912 | tf_op jit(solution)/shard_map/all_to_all | solution.py:193
  178.5 144.7 %reduce-scatter.2.cloned.1.call-start = ((), (), s32[]{:S(2)}) async-start(), calls=%async_computation.4 | async-start | bytes 2359296 | tf_op jit(solution)/shard_map/reduce_scatter | solution.py:204
  271.5 11.1 %copy-start.9 = (bf16[256,256]{1,0:T(8,128)(2,1)S(1)}, bf16[256,256]{1,0:T(8,128)(2,1)}, u32[]{:S(2)}) copy-start(bf16[256,256]{1,0:T(8,128)(2,1)} %param.26) | copy-start | bytes 393220
  271.5 11.2 %copy-start.11 = (s32[256]{0:T(256)S(1)}, s32[256]{0:T(256)}, u32[]{:S(2)}) copy-start(s32[256]{0:T(256)} %param.19) | copy-start | bytes 3076
  271.5 13.1 %copy-start.8 = (bf16[256,256]{1,0:T(8,128)(2,1)S(1)}, bf16[256,256]{1,0:T(8,128)(2,1)}, u32[]{:S(2)}) copy-start(bf16[256,256]{1,0:T(8,128)(2,1)} %param.27) | copy-start | bytes 393220
  271.5 14.0 %copy-start.10 = (bf16[256,256]{1,0:T(8,128)(2,1)S(1)}, bf16[256,256]{1,0:T(8,128)(2,1)}, u32[]{:S(2)}) copy-start(bf16[256,256]{1,0:T(8,128)(2,1)} %param.25) | copy-start | bytes 393220
  271.5 54.9 %copy-start.13 = (u32[256]{0:T(256)S(1)}, u32[256]{0:T(256)}, u32[]{:S(2)}) copy-start(u32[256]{0:T(256)} %constant.198) | copy-start | bytes 3076
  271.6 127.9 %copy-start.6 = (bf16[1,32,48,256]{3,2,1,0:T(8,128)(2,1)S(1)}, bf16[1,32,48,256]{3,2,1,0:T(8,128)(2,1)}, u32[]{:S(2)}) copy-start(bf16[1,32,48,256]{3,2,1,0:T(8,128)(2,1)} %param.20) | copy-start | bytes 2359300
  282.4 118.8 %all-gather.5.cloned.1.call-start = ((), (), s32[]{:S(2)}) async-start(), calls=%async_computation.5 | async-start | bytes 2162688 | tf_op jit(solution)/shard_map/all_gather | solution.py:17
  285.5 128.4 %all-gather.7.cloned.1.call-start = ((), (), s32[]{:S(2)}) async-start(), calls=%async_computation.6 | async-start | bytes 2162688 | tf_op jit(solution)/shard_map/all_gather | solution.py:17
  406.5 169.7 %copy-start.1 = (bf16[1,2048,256]{2,1,0:T(8,128)(2,1)S(1)}, bf16[1,2048,256]{2,1,0:T(8,128)(2,1)}, u32[]{:S(2)}) copy-start(bf16[1,2048,256]{2,1,0:T(8,128)(2,1)} %param.22) | copy-start | bytes 3145732
Sparse Core Ops, SparseCore 0:
  282.5 40.6 reduce-scatter.1
Sparse Core Ops, SparseCore 1:
  286.0 52.2 all-gather.4
  341.3 48.2 all-gather.6
where the time goes:
time: 587 us; the launch traced here: 584 us
  waiting for transfers between devices  183 us (31%)
  local copies, waits for them, and re-layouts  117 us (20%)
  loops' own time  82.3 us (14%)
  other arithmetic  71.3 us (12%)
  blocking collectives  67.1 us (11%)
  starting transfers between devices  26.1 us (4%)
  matrix products  19 us (3%)
  between operations  17.3 us (3%)
    another operation x2, loops' own time, prefix(): return lax.fori_loop(0, ahead, one, state)  82.3 us
    all_to_all x1, waiting for transfers between devices, local(): lax.all_to_all(send_rows, 'ctx', split_axis=0, concat_axis=0, tiled=True)  72.9 us
    all_to_all x1, waiting for transfers between devices, local(): lax.all_to_all(input_part.reshape(owners, slot_count, model_width), 'ctx'...  72.6 us
    unnamed x1, blocking collectives  67.1 us
    dynamic_slice x93, local copies, waits for them, and re-layouts, one(): lax.dynamic_index_in_dim(a, source, 0, False).astype(own.dtype)  54.8 us
    reduce_scatter x1, waiting for transfers between devices, local(): lax.psum_scatter(token_sum, 'ep', scatter_dimension=1, tiled=True)  37.5 us
    add x31, other arithmetic, join_states(): state_b + jnp.where(carried[..., None, None, None], state_a, 0.0)  27.3 us
    gather x1, local copies, waits for them, and re-layouts, gather_back(): jnp.take(returned.reshape(-1, model_width), row_index, axis=0)  20 us
  transfers between devices with their start and end apart: 6, of which 3 were waited for; matrix products, arithmetic and copies ran while one was open for 8% of the time, Pallas kernels for 0%

commit v1 on v0

v1 whole, which is shorter than its diff:
```python
import jax
import jax.numpy as jnp
from jax import lax
from jax.sharding import PartitionSpec as P

HEAD_DIM = 128


def dot(a, b, dims, batch=((), ())):
    return lax.dot_general(a, b, (dims, batch), preferred_element_type=jnp.float32)


def dispatch_matrix(gate_values, expert_ids, parity, owners, slot_count):
    tokens, top_count = expert_ids.shape
    experts = 2 * jnp.arange(owners, dtype=jnp.int32) + parity
    hit = expert_ids.T[:, None, :] == experts[None, :, None]
    named = jnp.any(hit, axis=0)
    gate = jnp.sum(jnp.where(hit, gate_values.T.astype(jnp.float32)[:, None, :], 0.0), axis=0)
    places = jnp.arange(tokens, dtype=jnp.int32)
    earlier = (places[:, None] < places[None, :]).astype(jnp.bfloat16)
    before = dot(named.astype(jnp.bfloat16), earlier, ((1,), (0,)))
    rank = jnp.where(named, before, -1.0)
    slots = jnp.arange(slot_count, dtype=jnp.int32).astype(jnp.float32)
    seated = rank[:, None, :] == slots[None, :, None]
    return seated.astype(jnp.bfloat16), jnp.where(seated, gate[:, None, :], 0.0).astype(jnp.bfloat16)


def expert_rows(cotangent, pre_gate, pre_up, gate_matrix, up_matrix, down_matrix):
    down_part = dot(cotangent, down_matrix, ((1,), (1,)))
    gate_value = pre_gate.astype(jnp.float32)
    up_value = pre_up.astype(jnp.float32)
    sigmoid_gate = jax.nn.sigmoid(gate_value)
    hidden = (gate_value * sigmoid_gate * up_value).astype(jnp.bfloat16)
    down_grad = dot(hidden, cotangent, ((0,), (0,)))
    gate_delta = (
        down_part * up_value * sigmoid_gate * (1.0 + gate_value * (1.0 - sigmoid_gate))
    ).astype(jnp.bfloat16)
    up_delta = (down_part * gate_value * sigmoid_gate).astype(jnp.bfloat16)
    input_part = dot(gate_delta, gate_matrix, ((1,), (1,))) + dot(up_delta, up_matrix, ((1,), (1,)))
    return input_part.astype(jnp.bfloat16), down_grad


def local(
    out_grad,
    gate_values,
    expert_ids,
    segment_ids,
    gate_pre,
    up_pre,
    w_gate,
    w_up,
    w_down,
    queries,
    keys,
    values,
):
    owners = lax.axis_size("ctx")
    groups = lax.axis_size("ep")
    here = lax.axis_index("ctx")
    parity = lax.axis_index("ep") // (groups // 2)
    tokens, width = out_grad.shape
    slot_count = gate_pre.shape[2]
    rows = owners * slot_count
    bf16 = jnp.bfloat16

    heads = queries.shape[1] // HEAD_DIM
    shape = (tokens, heads, HEAD_DIM)
    query3, key3, value3 = (a.reshape(shape).transpose(1, 0, 2) for a in (queries, keys, values))
    first_doc = (segment_ids == segment_ids[0]).astype(bf16)
    last_doc = (segment_ids == segment_ids[-1]).astype(bf16)
    ends = lax.all_gather(jnp.stack([segment_ids[0], segment_ids[-1]]), "ctx")
    order = jnp.arange(owners, dtype=jnp.int32)
    from_before = ((ends[:, 1] == segment_ids[0]) & (order < here)).astype(jnp.float32)
    from_after = ((ends[:, 0] == segment_ids[-1]) & (order > here)).astype(jnp.float32)
    per_head = ((0,), (0,))
    forward = dot(key3 * last_doc[None, :, None], value3, ((1,), (1,)), per_head)
    forwards = lax.all_gather(forward.astype(bf16), "ctx").astype(jnp.float32)
    state_in = jnp.sum(forwards * from_before[:, None, None, None], axis=0).astype(bf16)

    seated, weighted = dispatch_matrix(gate_values, expert_ids, parity, owners, slot_count)
    send = dot(weighted.reshape(rows, tokens), out_grad, ((1,), (0,))).astype(bf16)
    cotangent = lax.all_to_all(send, "ctx", split_axis=0, concat_axis=0, tiled=True)
    input_part, down_grad = expert_rows(
        cotangent,
        gate_pre[0].reshape(rows, -1),
        up_pre[0].reshape(rows, -1),
        w_gate[0],
        w_up[0],
        w_down[0],
    )
    returned = lax.all_to_all(input_part, "ctx", split_axis=0, concat_axis=0, tiled=True)
    token_sum = dot(seated.reshape(rows, tokens), returned, ((0,), (0,))).astype(bf16)
    parts = lax.all_to_all(token_sum, "ep", split_axis=1, concat_axis=0, tiled=True)
    head_cot = jnp.sum(parts.reshape(groups, tokens, -1).astype(jnp.float32), axis=0).astype(bf16)
    cot3 = head_cot.reshape(shape).transpose(1, 0, 2)

    backward = dot(query3 * first_doc[None, :, None], cot3, ((1,), (1,)), per_head)
    backwards = lax.all_gather(backward.astype(bf16), "ctx").astype(jnp.float32)
    back_in = jnp.sum(backwards * from_after[:, None, None, None], axis=0).astype(bf16)

    places = jnp.arange(tokens, dtype=jnp.int32)
    allowed = (places[:, None] >= places[None, :]) & (segment_ids[:, None] == segment_ids[None, :])
    cot_value = jnp.where(allowed[None], dot(cot3, value3, ((2,), (2,)), per_head), 0.0).astype(bf16)
    query_key = jnp.where(allowed[None], dot(query3, key3, ((2,), (2,)), per_head), 0.0).astype(bf16)
    query_grad = dot(cot_value, key3, ((2,), (1,)), per_head)
    key_grad = dot(cot_value, query3, ((1,), (1,)), per_head)
    value_grad = dot(query_key, cot3, ((1,), (1,)), per_head)
    query_grad += dot(cot3 * first_doc[None, :, None], state_in, ((2,), (2,)), per_head)
    key_grad += dot(value3 * last_doc[None, :, None], back_in, ((2,), (2,)), per_head)
    value_grad += dot(key3 * last_doc[None, :, None], back_in, ((2,), (1,)), per_head)

    def flat(a):
        return a.astype(bf16).transpose(1, 0, 2).reshape(tokens, -1)

    return flat(query_grad), flat(key_grad), flat(value_grad), down_grad[None]


def solution(mesh):
    row, col = P("ctx", None), P("ctx", "ep")
    both = ("ctx", "ep")
    pre, weight = P(both, None, None, None), P(both, None, None)
    return jax.shard_map(
        local,
        mesh=mesh,
        in_specs=(row, row, row, P("ctx"), pre, pre, weight, weight, weight, col, col, col),
        out_specs=(col, col, col, weight),
        check_vma=False,
    )
```

time: 587 us -> 284 us (0.48)
  local copies, waits for them, and re-layouts: 117 us -> 5.14 us
  loops' own time: 82.3 us -> 0 us
  waiting for transfers between devices: 183 us -> 113 us
  other arithmetic: 71.3 us -> 13 us
  blocking collectives: 67.1 us -> 98.9 us
  starting transfers between devices: 26.1 us -> 13.7 us
  matrix products: 19 us -> 25 us
    another operation x2 -> x0, loops' own time: 82.3 us -> none  [prefix(): return lax.fori_loop(0, ahead, one, state)]
    all_to_all x0 -> x1, blocking collectives: none -> 81.9 us  [local(): lax.all_to_all(send, 'ctx', split_axis=0, concat_axis=0, tiled=True)]
    dynamic_slice x93 -> x0, local copies, waits for them, and re-layouts: 54.8 us -> none  [one(): lax.dynamic_index_in_dim(a, source, 0, False).astype(own.dtype)]
    unnamed x1, blocking collectives: 67.1 us -> 17.1 us
    all_to_all x3 -> x2, waiting for transfers between devices: 146 us -> 96 us  [the longest x1 71.3 us: local(): lax.all_to_all(input_part, 'ctx', split_axis=0, concat_axis=0, tiled=True)]
    reduce_scatter x1 -> x0, waiting for transfers between devices: 37.5 us -> none  [local(): lax.psum_scatter(token_sum, 'ep', scatter_dimension=1, tiled=True)]
    add x31 -> x1, other arithmetic: 27.3 us -> 0.01 us  [dispatch_matrix(): experts = 2 * jnp.arange(owners, dtype=jnp.int32) + parity]
    gather x2 -> x0, local copies, waits for them, and re-layouts: 27.1 us -> none  [the longest x1 20 us: gather_back(): jnp.take(returned.reshape(-1, model_width), row_index, axis=0)]
  transfers between devices with their start and end apart: 6 -> 4, of which waited for: 3 -> 3; matrix products, arithmetic and copies ran while one was open for 8% -> 9% of each run, Pallas kernels for 0% -> 0%
where the time goes in v1:
time: 284 us
  waiting for transfers between devices  113 us (40%)
  blocking collectives  98.9 us (35%)
  matrix products  25 us (9%)
  between operations  15 us (5%)
  starting transfers between devices  13.7 us (5%)
  other arithmetic  13 us (5%)
  local copies, waits for them, and re-layouts  5.14 us (2%)
    all_to_all x1, blocking collectives, local(): lax.all_to_all(send, 'ctx', split_axis=0, concat_axis=0, tiled=True)  81.9 us
    all_to_all x1, waiting for transfers between devices, local(): lax.all_to_all(input_part, 'ctx', split_axis=0, concat_axis=0, tiled=True)  71.3 us
    dot_general x16, matrix products, dot(): lax.dot_general(a, b, (dims, batch), preferred_element_type=jnp.float32)  25 us
    all_to_all x1, waiting for transfers between devices, local(): lax.all_to_all(token_sum, 'ep', split_axis=1, concat_axis=0, tiled=True)  24.8 us
    unnamed x1, blocking collectives  17.1 us
    all_gather x1, waiting for transfers between devices, local(): backwards = lax.all_gather(backward.astype(bf16), 'ctx').astype(jnp.float32)  16.7 us
    all_to_all x1, starting transfers between devices, local(): lax.all_to_all(token_sum, 'ep', split_axis=1, concat_axis=0, tiled=True)  8.44 us
  transfers between devices with their start and end apart: 4, of which 3 were waited for; matrix products, arithmetic and copies ran while one was open for 9% of the time, Pallas kernels for 0%

profile of v1, /device:TPU:1, one launch (start us, length us, event | category | flops | bytes accessed | tf_op | source)
XLA Modules:
  0.0 283.7 jit_solution(2571117110902228074)
XLA Ops:
  7.2 0.0 copy-start
  7.2 0.8 convert_bitcast_fusion
  8.0 0.8 compare_reduce_fusion
  8.8 0.8 fusion.32
  9.6 0.1 eq.103
  9.7 0.1 convolution_select_fusion.2
  9.8 0.3 fusion.16
  10.1 0.0 copy-done
  10.1 1.8 convolution_convert_fusion
  11.9 0.0 copy-start.4
  12.0 0.0 copy-start.5
  12.0 0.0 copy-start.10
  12.0 81.9 %all_to_all.34 = bf16[32,48,2048]{2,1,0:T(8,128)(2,1)S(1)} all-to-all(bf16[32,48,2048]{2,1,0:T(8,128)(2,1)S(1)} %bitcast.167), channel_id=1, replica_groups=mesh['ctx'=32,'ep'=8] {'ctx'}, dimensions={0} | all-to-all | bytes 12582912 | tf_op jit(solution)/shard_map/all_to_all | solution.py:82
  93.9 0.0 copy-done.4
  93.9 0.0 copy-done.5
  93.9 0.0 copy-done.10
  93.9 0.0 copy-start.2
  93.9 2.5 fusion.14
  96.4 0.1 copy-done.1
  96.5 0.0 copy-done.2
  96.5 1.8 fusion.26
  98.3 0.0 copy-done.3
  98.4 4.4 %add_convert_fusion = bf16[1536,2048]{1,0:T(8,128)(2,1)} fusion(f32[1536,2048]{1,0:T(8,128)S(1)} %fusion.26, bf16[1536,256]{1,0:T(8,128)(2,1)S(1)} %get-tuple-element.22, bf16[1,2048,256]{2,1,0:T(8,128)(2,1)S(1)} %copy-done.3), kind=kOutput, calls=%fused_computation | convolution fusion | flops 1616904192 | bytes 20709376 | tf_op jit(solution)/shard_map/dot_general | solution.py:10
  102.8 5.0 %all-to-all-start.1 = ((bf16[32,48,2048]{2,1,0:T(8,128)(2,1)}), bf16[32,48,2048]{2,1,0:T(8,128)(2,1)}, u32[]{:S(2)}, u32[]{:S(2)}) async-start(bf16[32,48,2048]{2,1,0:T(8,128)(2,1)} %bitcast.168), calls=%async_computation.1 | async-start | bytes 12582912 | tf_op jit(solution)/shard_map/all_to_all | solution.py:91
  107.8 0.0 all-gather.6.cloned.1.call-start
  107.9 0.0 copy-done.9
  107.9 0.7 fusion.64
  108.5 1.3 compare_convert_fusion.1
  109.9 0.9 convolution_convert_fusion.2
  110.8 0.0 all-gather.6.cloned.1.call-update
  110.8 71.3 %all-to-all-done.1 = bf16[32,48,2048]{2,1,0:T(8,128)(2,1)} async-done(((bf16[32,48,2048]{2,1,0:T(8,128)(2,1)}), bf16[32,48,2048]{2,1,0:T(8,128)(2,1)}, u32[]{:S(2)}, u32[]{:S(2)}) %all-to-all-start.1) | async-done | bytes 6291488 | tf_op jit(solution)/shard_map/all_to_all | solution.py:91
  182.1 4.9 %fusion.2 = bf16[256,2048]{1,0:T(8,128)(2,1)S(1)} fusion(bf16[32,48,2048]{2,1,0:T(8,128)(2,1)} %all-to-all-done.1, f32[32,256]{1,0:T(8,128)S(1)} %convolution_select_fusion.2, f32[48]{0:T(128)S(1)} %iota_convert_fusion), kind=kOutput, calls=%fused_computation.8 | convolution fusion | flops 1611530240 | bytes 7372992 | tf_op jit(solution)/shard_map/dot_general | solution.py:10
  187.0 0.0 copy-start.7
  187.0 1.0 copy.117
  188.0 8.4 %all-to-all-start.2 = ((bf16[256,8,256]{2,0,1:T(8,128)(2,1)}), bf16[256,8,256]{2,0,1:T(8,128)(2,1)S(1)}, u32[]{:S(2)}, u32[]{:S(2)}) async-start(bf16[256,8,256]{2,0,1:T(8,128)(2,1)} %bitcast.164), calls=%async_computation.2 | async-start | bytes 2097152 | tf_op jit(solution)/shard_map/all_to_all | solution.py:93
  196.5 0.2 all-gather.8.cloned.1.call-start
  196.7 0.1 copy.82
  196.8 24.8 %all-to-all-done.2 = bf16[256,8,256]{2,0,1:T(8,128)(2,1)S(1)} async-done(((bf16[256,8,256]{2,0,1:T(8,128)(2,1)}), bf16[256,8,256]{2,0,1:T(8,128)(2,1)S(1)}, u32[]{:S(2)}, u32[]{:S(2)}) %all-to-all-start.2) | async-done | bytes 1048608 | tf_op jit(solution)/shard_map/all_to_all | solution.py:93
  221.6 0.1 reduce_sum.40
  221.7 0.1 copy.79
  221.8 0.8 convolution_convert_fusion.1
  222.7 0.0 all-gather.8.cloned.1.call-update
  222.7 0.6 dynamic-slice
  224.0 1.5 add_dynamic-update-slice_fusion
  225.4 17.1 %all-reduce = s32[64]{0:T(128)S(1)} all-reduce(s32[64]{0:T(128)S(1)} %add_dynamic-update-slice_fusion), channel_id=3, replica_groups=mesh['ctx'=32,'ep'=8] {'ctx'}, use_global_device_ids=true, to_apply=%add | all-reduce | flops 64 | bytes 512
  242.5 0.1 reshape.139
  242.6 1.5 fusion.62
  244.1 0.1 fusion.34
  244.2 1.6 fusion.17
  245.9 0.0 all-gather.6.cloned.1.call-done
  245.9 2.1 fusion.1
  248.0 5.9 %convolution_bitcast_fusion = f32[1,256,2048]{2,1,0:T(8,128)} fusion(bf16[1536,256]{1,0:T(8,128)(2,1)S(1)} %bitcast.169, bf16[1536,2048]{1,0:T(8,128)(2,1)} %bitcast.166), kind=kOutput, calls=%fused_computation.6 | convolution fusion | flops 1610612736 | bytes 9175040 | tf_op jit(solution)/shard_map/dot_general | solution.py:10
  253.9 0.3 fusion.19
  254.2 0.2 fusion.37
  254.4 0.2 fusion.23
  254.6 0.8 copy.69
  255.4 0.4 fusion.21
  255.8 16.7 %all-gather.8.cloned.1.call-done = bf16[64,128,128]{2,1,0:T(8,128)(2,1)} async-done(((bf16[2,128,128]{2,1,0:T(8,128)(2,1)}), bf16[64,128,128]{2,1,0:T(8,128)(2,1)}) %all-gather.8.cloned.1.call-update) | async-done | bytes 2097168 | tf_op jit(solution)/shard_map/all_gather | solution.py:98
  272.5 2.1 fusion
  274.6 0.3 fusion.39
  274.9 0.3 fusion.22
  275.2 0.8 copy.71
  275.9 0.2 fusion.24
  276.1 0.8 copy.70
  (16 shorter events, 0.0 us)
Async XLA Ops:
  7.2 3.0 %copy-start = (bf16[256,2048]{1,0:T(8,128)(2,1)S(1)}, bf16[256,2048]{1,0:T(8,128)(2,1)}, u32[]{:S(2)}) copy-start(bf16[256,2048]{1,0:T(8,128)(2,1)} %param.12) | copy-start | bytes 3145732
  11.9 81.9 %copy-start.4 = (bf16[1,32,48,256]{3,2,1,0:T(8,128)(2,1)S(1)}, bf16[1,32,48,256]{3,2,1,0:T(8,128)(2,1)}, u32[]{:S(2)}) copy-start(bf16[1,32,48,256]{3,2,1,0:T(8,128)(2,1)} %param.16) | copy-start | bytes 2359300
  12.0 81.9 %copy-start.5 = (bf16[1,32,48,256]{3,2,1,0:T(8,128)(2,1)S(1)}, bf16[1,32,48,256]{3,2,1,0:T(8,128)(2,1)}, u32[]{:S(2)}) copy-start(bf16[1,32,48,256]{3,2,1,0:T(8,128)(2,1)} %param.17) | copy-start | bytes 2359300
  12.0 81.9 %copy-start.10 = (bf16[1,256,2048]{2,1,0:T(8,128)(2,1)S(1)}, bf16[1,256,2048]{2,1,0:T(8,128)(2,1)}, u32[]{:S(2)}) copy-start(bf16[1,256,2048]{2,1,0:T(8,128)(2,1)} %param.20) | copy-start | bytes 3145732
  93.9 2.6 copy-start.1
  93.9 2.6 copy-start.2
  96.5 1.8 copy-start.3
  102.8 5.1 %copy-start.9 = (s32[256]{0:T(256)S(1)}, s32[256]{0:T(256)}, u32[]{:S(2)}) copy-start(s32[256]{0:T(256)} %param.15) | copy-start | bytes 3076
  102.8 7.1 %copy-start.6 = (bf16[256,256]{1,0:T(8,128)(2,1)S(1)}, bf16[256,256]{1,0:T(8,128)(2,1)}, u32[]{:S(2)}) copy-start(bf16[256,256]{1,0:T(8,128)(2,1)} %param.22) | copy-start | bytes 393220
  102.8 7.1 %copy-start.8 = (bf16[256,256]{1,0:T(8,128)(2,1)S(1)}, bf16[256,256]{1,0:T(8,128)(2,1)}, u32[]{:S(2)}) copy-start(bf16[256,256]{1,0:T(8,128)(2,1)} %param.23) | copy-start | bytes 393220
  102.8 79.3 %all-to-all-start.1 = ((bf16[32,48,2048]{2,1,0:T(8,128)(2,1)}), bf16[32,48,2048]{2,1,0:T(8,128)(2,1)}, u32[]{:S(2)}, u32[]{:S(2)}) async-start(bf16[32,48,2048]{2,1,0:T(8,128)(2,1)} %bitcast.168), calls=%async_computation.1 | async-start | bytes 12582912 | tf_op jit(solution)/shard_map/all_to_all | solution.py:91
  107.8 138.1 %all-gather.6.cloned.1.call-start = ((), (), s32[]{:S(2)}) async-start(), calls=%async_computation.3 | async-start | bytes 2162688 | tf_op jit(solution)/shard_map/all_gather | solution.py:77
  187.0 9.7 %copy-start.7 = (bf16[256,256]{1,0:T(8,128)(2,1)S(1)}, bf16[256,256]{1,0:T(8,128)(2,1)}, u32[]{:S(2)}) copy-start(bf16[256,256]{1,0:T(8,128)(2,1)} %param.21) | copy-start | bytes 393220
  188.0 34.7 %copy-start.11 = (u32[256]{0:T(256)S(1)}, u32[256]{0:T(256)}, u32[]{:S(2)}) copy-start(u32[256]{0:T(256)} %constant.43) | copy-start | bytes 3076
  188.0 33.6 %all-to-all-start.2 = ((bf16[256,8,256]{2,0,1:T(8,128)(2,1)}), bf16[256,8,256]{2,0,1:T(8,128)(2,1)S(1)}, u32[]{:S(2)}, u32[]{:S(2)}) async-start(bf16[256,8,256]{2,0,1:T(8,128)(2,1)} %bitcast.164), calls=%async_computation.2 | async-start | bytes 2097152 | tf_op jit(solution)/shard_map/all_to_all | solution.py:93
  196.5 76.1 %all-gather.8.cloned.1.call-start = ((), (), s32[]{:S(2)}) async-start(), calls=%async_computation.4 | async-start | bytes 2162688 | tf_op jit(solution)/shard_map/all_gather | solution.py:98
Sparse Core Ops, SparseCore 0:
  111.8 86.1 all-gather.5
  222.8 49.6 all-gather.7

commit v2 on v1

v2 whole, which is shorter than its diff:
```python
import jax
import jax.numpy as jnp
from jax import lax
from jax.experimental import pallas as pl
from jax.experimental.pallas import tpu as pltpu
from jax.sharding import PartitionSpec as P

HEAD_DIM = 128
MESH = pl.DeviceIdType.MESH
BF16, F32, I32 = jnp.bfloat16, jnp.float32, jnp.int32
OWNERS, GROUPS = 32, 8
SLOTS, TOKENS, WIDTH, HIDDEN = 48, 256, 2048, 256
TAKE, SHARE = 1280, 768
FIRST, SPAN, BLOCKS = WIDTH - TAKE, 256, TAKE // 256
STEP = 4
STEPS, ROWS = OWNERS // STEP, STEP * SLOTS
REACH = 7


def dot(a, b, dims):
    return lax.dot_general(a, b, (dims, ((), ())), preferred_element_type=F32)


def place(me):
    return me // 8, (me // 2) % 4, me % 2


def offset(slot):
    o = (11 * slot) % 32
    return o // 8, (o // 2) % 4, o % 2


def dest(me, slot):
    (y, x, c), (dy, dx, dc) = place(me), offset(slot)
    a, b = dy + c * (dx - dy), dx + c * (dy - dx)
    return ((y + a) % 4) * 8 + ((x + b) % 4) * 2 + (c + dc) % 2


def source(me, slot):
    (y, x, c), (dy, dx, dc) = place(me), offset(slot)
    s = (c + dc) % 2
    a, b = dy + s * (dx - dy), dx + s * (dy - dx)
    return ((y + 4 - a) % 4) * 8 + ((x + 4 - b) % 4) * 2 + s


def kernel(
    rank, gate, rows_in, gate_pre, up_pre, w_gate, w_up, w_down, q_ref, k_ref, v_ref, seg_row, seg_col, ends,
    q_out, k_out, v_out, down_out,
    send, cot, part, part_in, back, got, hidden, y_sum, y_out, y_in, y_acc, state_out, state_in, ends_in, scores, carried,
    send_s, send_r, pass_s, pass_r, pair_s, pair_r, back_s, back_r, y_s, y_r, state_s, state_r, ends_s, ends_r,
):
    me, z = lax.axis_index("ctx"), lax.axis_index("ep")
    half = z % 2
    mate = z + 1 - 2 * half
    base = pl.multiple_of(half * FIRST, 128)
    mine = pl.multiple_of(half * TAKE, 128)
    theirs = pl.multiple_of((1 - half) * TAKE, 128)

    def remote(src, dst, s, r, ctx, ep):
        return pltpu.make_async_remote_copy(src, dst, s, r, device_id=(ctx, ep), device_id_type=MESH)

    def sending(i):
        return remote(send.at[i], cot.at[i, :, pl.ds(base, TAKE)], send_s.at[i], send_r.at[i], dest(me, i), z)

    def passing(i):
        columns = cot.at[i, :, pl.ds(mine, SHARE)]
        return remote(columns, columns, pass_s.at[i], pass_r.at[i], me, mate)

    def passed(i):
        columns = cot.at[i, :, pl.ds(theirs, SHARE)]
        return remote(columns, columns, pass_s.at[i], pass_r.at[i], me, mate)

    def pairing(i):
        return remote(part.at[i, :, pl.ds(theirs, SHARE)], part_in.at[i], pair_s.at[i], pair_r.at[i], me, mate)

    def returning(i):
        return remote(back.at[i], got.at[i], back_s.at[i], back_r.at[i], source(me, i), z)

    def shard(j):
        return (me + 1 + j) % OWNERS if j < REACH else (me + OWNERS - (j - REACH + 1)) % OWNERS

    def telling(j):
        return remote(ends, ends_in.at[j], ends_s.at[j], ends_r.at[j], shard(j), z)

    def stating(j):
        return remote(state_out.at[j // REACH], state_in.at[j], state_s.at[j], state_r.at[j], shard(j), z)

    barrier = pltpu.get_barrier_semaphore()

    @pl.loop(1, OWNERS)
    def _(i):
        pl.semaphore_signal(barrier, 1, device_id=((me + i) % OWNERS, z), device_id_type=MESH)

    @pl.loop(1, GROUPS)
    def _(i):
        pl.semaphore_signal(barrier, 1, device_id=(me, (z + i) % GROUPS), device_id_type=MESH)

    slot_of = lax.broadcasted_iota(I32, (SLOTS, TOKENS), 0).astype(F32)

    def seats(g, weighted):
        blocks = []
        for j in range(STEP):
            seated = slot_of == rank[g * STEP + j]
            blocks.append(jnp.where(seated, gate[g * STEP + j] if weighted else 1.0, 0.0).astype(BF16))
        return jnp.concatenate(blocks, axis=0)

    def fill(g):
        made = dot(seats(g, True), rows_in[:, pl.ds(base, TAKE)], ((1,), (0,)))
        send[pl.ds(g * STEP, STEP)] = made.astype(BF16).reshape(STEP, SLOTS, TAKE)

    fill(0)
    pl.semaphore_wait(barrier, OWNERS + GROUPS - 2)

    for j in range(2 * REACH):
        telling(j).start()

    @pl.loop(0, STEPS)
    def _(g):
        @pl.when(g > 0)
        def _():
            fill(g)

        for j in range(STEP):

            @pl.when(g * STEP + j > 0)
            def _():
                sending(g * STEP + j).start()

    own = jnp.where(slot_of == rank[0], gate[0], 0.0).astype(BF16)
    cot[0] = dot(own, rows_in[...], ((1,), (0,))).astype(BF16)

    first_mask = seg_col[...] == ends[0:1, :]
    last_mask = seg_col[...] == ends[8:9, :]
    for h in range(2):
        head = slice(h * HEAD_DIM, (h + 1) * HEAD_DIM)
        held = jnp.where(last_mask, k_ref[:, head].astype(F32), 0.0).astype(BF16)
        state_out[0, h] = dot(held, v_ref[:, head], ((0,), (0,))).astype(BF16)
    for j in range(REACH):
        stating(j).start()

    def experts(g):
        these = pl.ds(g * STEP, STEP)
        rows = cot[these].reshape(ROWS, WIDTH)
        down_part = dot(rows, w_down[0], ((1,), (1,)))
        a = jnp.concatenate([gate_pre[0, source(me, g * STEP + j)] for j in range(STEP)], axis=0).astype(F32)
        u = jnp.concatenate([up_pre[0, source(me, g * STEP + j)] for j in range(STEP)], axis=0).astype(F32)
        s = jax.nn.sigmoid(a)
        hidden[pl.ds(g * ROWS, ROWS), :] = (a * s * u).astype(BF16)
        gate_delta = (down_part * u * s * (1.0 + a * (1.0 - s))).astype(BF16)
        up_delta = (down_part * a * s).astype(BF16)
        for n in range(WIDTH // 512):
            columns = slice(n * 512, (n + 1) * 512)
            total = dot(gate_delta, w_gate[0, columns, :], ((1,), (1,)))
            total += dot(up_delta, w_up[0, columns, :], ((1,), (1,)))
            part[these, :, columns] = total.astype(BF16).reshape(STEP, SLOTS, 512)

    @pl.loop(0, STEPS + 2)
    def _(t):
        @pl.when(t < STEPS)
        def _():
            for j in range(STEP):

                @pl.when(t * STEP + j > 0)
                def _():
                    sending(t * STEP + j).wait_recv()
                    passing(t * STEP + j).start()

        @pl.when((t > 0) & (t < STEPS + 1))
        def _():
            g = t - 1
            for j in range(STEP):

                @pl.when(g * STEP + j > 0)
                def _():
                    passed(g * STEP + j).wait_recv()

            experts(g)
            for j in range(STEP):
                pairing(g * STEP + j).start()

        @pl.when(t > 1)
        def _():
            g = t - 2
            for j in range(STEP):
                pairing(g * STEP + j).wait_recv()
            these = pl.ds(g * STEP, STEP)
            shared = pl.multiple_of(half * (TAKE - SHARE), 128)
            both = pl.multiple_of((1 - half) * SHARE, 128)
            summed = part[these, :, pl.ds(mine, SHARE)].astype(F32) + part_in[these].astype(F32)
            back[these, :, pl.ds(shared, SHARE)] = summed.astype(BF16)
            back[these, :, pl.ds(both, TAKE - SHARE)] = part[these, :, pl.ds(SHARE, TAKE - SHARE)]
            for j in range(STEP):

                @pl.when(g * STEP + j > 0)
                def _():
                    returning(g * STEP + j).start()

    got[0] = back[0]
    for n in range(WIDTH // 256):
        columns = slice(n * 256, (n + 1) * 256)
        down_out[0, :, columns] = dot(
            hidden[...], cot[:, :, columns].reshape(OWNERS * SLOTS, 256), ((0,), (0,))
        )

    rows_at = lax.broadcasted_iota(I32, (TOKENS, TOKENS), 0)
    cols_at = lax.broadcasted_iota(I32, (TOKENS, TOKENS), 1)
    allowed = (rows_at >= cols_at) & (jnp.concatenate([seg_col[...]] * 2, axis=1) == seg_row[0:1, :])

    def arrived(backward):
        total = jnp.zeros((2, HEAD_DIM, HEAD_DIM), F32)
        for j in range(REACH):
            k = backward * REACH + j
            stating(k).wait_recv()
            if backward:
                same = ends_in[k, 0:1, :] == ends[8:9, :]
                inside = jnp.where(me + 1 + j < OWNERS, 1.0, 0.0)
            else:
                same = ends_in[k, 8:9, :] == ends[0:1, :]
                inside = jnp.where(me - 1 - j >= 0, 1.0, 0.0)
            weight = jnp.where(same, 1.0, 0.0) * inside
            total += state_in[k].astype(F32) * weight[None]
        return total.astype(BF16)

    for j in range(2 * REACH):
        telling(j).wait_recv()
    carried[...] = arrived(0)
    for h in range(2):
        head = slice(h * HEAD_DIM, (h + 1) * HEAD_DIM)
        scores[h] = jnp.where(allowed, dot(q_ref[:, head], k_ref[:, head], ((1,), (1,))), 0.0).astype(BF16)

    y_sum[...] = jnp.zeros_like(y_sum)

    @pl.loop(0, STEPS)
    def _(g):
        for j in range(STEP):

            @pl.when(g * STEP + j > 0)
            def _():
                returning(g * STEP + j).wait_recv()

        rows = got[pl.ds(g * STEP, STEP)].reshape(ROWS, TAKE)
        y_sum[...] += dot(seats(g, False), rows, ((0,), (0,)))

    def spreading(b):
        to = 3 * half + b
        return remote(y_out.at[b], y_in.at[z], y_s.at[b], y_r.at[z], me, to)

    def spread(i):
        return remote(y_out.at[0], y_in.at[i], y_s.at[0], y_r.at[i], me, z)

    y_acc[...] = jnp.zeros_like(y_acc)
    for b in range(BLOCKS):
        block = y_sum[:, b * SPAN : (b + 1) * SPAN]
        y_out[b] = block.astype(BF16)

        @pl.when(3 * half + b != z)
        def _():
            spreading(b).start()

        @pl.when(3 * half + b == z)
        def _():
            y_acc[...] = y_sum[:, b * SPAN : (b + 1) * SPAN]

    for i in range(GROUPS):
        low = 3 * (i % 2)

        @pl.when((z != i) & (z >= low) & (z < low + BLOCKS))
        def _():
            spread(i).wait_recv()
            y_acc[...] += y_in[i].astype(F32)

    for h in range(2):
        head = slice(h * HEAD_DIM, (h + 1) * HEAD_DIM)
        opened = jnp.where(first_mask, q_ref[:, head].astype(F32), 0.0).astype(BF16)
        state_out[1, h] = dot(opened, y_acc[:, head].astype(BF16), ((0,), (0,))).astype(BF16)
    for j in range(REACH, 2 * REACH):
        stating(j).start()

    inner = []
    for h in range(2):
        head = slice(h * HEAD_DIM, (h + 1) * HEAD_DIM)
        g_h = y_acc[:, head].astype(BF16)
        cot_value = jnp.where(allowed, dot(g_h, v_ref[:, head], ((1,), (1,))), 0.0).astype(BF16)
        query_grad = dot(cot_value, k_ref[:, head], ((1,), (0,)))
        query_grad += jnp.where(first_mask, dot(g_h, carried[h], ((1,), (1,))), 0.0)
        q_out[:, head] = query_grad.astype(BF16)
        inner.append((dot(cot_value, q_ref[:, head], ((0,), (0,))), dot(scores[h], g_h, ((0,), (0,)))))

    back_state = arrived(1)
    for h in range(2):
        head = slice(h * HEAD_DIM, (h + 1) * HEAD_DIM)
        key_grad, value_grad = inner[h]
        key_part = dot(v_ref[:, head], back_state[h], ((1,), (1,)))
        value_part = dot(k_ref[:, head], back_state[h], ((1,), (0,)))
        k_out[:, head] = (key_grad + jnp.where(last_mask, key_part, 0.0)).astype(BF16)
        v_out[:, head] = (value_grad + jnp.where(last_mask, value_part, 0.0)).astype(BF16)

    pairing(0).wait_send()

    @pl.loop(1, OWNERS)
    def _(i):
        sending(i).wait_send()
        passing(i).wait_send()
        pairing(i).wait_send()
        returning(i).wait_send()

    for b in range(BLOCKS):

        @pl.when(3 * half + b != z)
        def _():
            spreading(b).wait_send()

    for j in range(2 * REACH):
        telling(j).wait_send()
        stating(j).wait_send()


def local(
    out_grad, gate_values, expert_ids, segment_ids, gate_pre, up_pre, w_gate, w_up, w_down, queries, keys, values
):
    me = lax.axis_index("ctx")
    parity = lax.axis_index("ep") // (GROUPS // 2)
    experts = 2 * dest(me, jnp.arange(OWNERS, dtype=I32)) + parity
    hit = expert_ids.T[:, None, :] == experts[None, :, None]
    named = jnp.any(hit, axis=0)
    gate = jnp.sum(jnp.where(hit, gate_values.T.astype(F32)[:, None, :], 0.0), axis=0)
    places = jnp.arange(TOKENS, dtype=I32)
    earlier = (places[:, None] < places[None, :]).astype(BF16)
    rank = jnp.where(named, dot(named.astype(BF16), earlier, ((1,), (0,))), -1.0)
    seg_row = jnp.broadcast_to(segment_ids[None, :], (8, TOKENS))
    seg_col = jnp.broadcast_to(segment_ids[:, None], (TOKENS, 128))
    ends = jnp.concatenate([jnp.full((8, 128), segment_ids[0]), jnp.full((8, 128), segment_ids[-1])], axis=0)

    vmem = pl.BlockSpec(memory_space=pltpu.VMEM)
    dma = pltpu.SemaphoreType.DMA
    small = jax.ShapeDtypeStruct((TOKENS, SPAN), BF16)
    states = (2, HEAD_DIM, HEAD_DIM)
    return pl.pallas_call(
        kernel,
        out_shape=(small, small, small, jax.ShapeDtypeStruct((1, HIDDEN, WIDTH), F32)),
        in_specs=[vmem] * 14,
        out_specs=(vmem,) * 4,
        scratch_shapes=[
            pltpu.VMEM((OWNERS, SLOTS, TAKE), BF16),
            pltpu.VMEM((OWNERS, SLOTS, WIDTH), BF16),
            pltpu.VMEM((OWNERS, SLOTS, WIDTH), BF16),
            pltpu.VMEM((OWNERS, SLOTS, SHARE), BF16),
            pltpu.VMEM((OWNERS, SLOTS, TAKE), BF16),
            pltpu.VMEM((OWNERS, SLOTS, TAKE), BF16),
            pltpu.VMEM((OWNERS * SLOTS, HIDDEN), BF16),
            pltpu.VMEM((TOKENS, TAKE), F32),
            pltpu.VMEM((BLOCKS, TOKENS, SPAN), BF16),
            pltpu.VMEM((GROUPS, TOKENS, SPAN), BF16),
            pltpu.VMEM((TOKENS, SPAN), F32),
            pltpu.VMEM((2, *states), BF16),
            pltpu.VMEM((2 * REACH, *states), BF16),
            pltpu.VMEM((2 * REACH, 16, 128), I32),
            pltpu.VMEM((2, TOKENS, TOKENS), BF16),
            pltpu.VMEM(states, BF16),
            *[dma((OWNERS,))] * 8,
            dma((BLOCKS,)), dma((GROUPS,)), *[dma((2 * REACH,))] * 4,
        ],
        compiler_params=pltpu.CompilerParams(
            collective_id=0, has_side_effects=True, vmem_limit_bytes=58 << 20
        ),
    )(
        rank[:, None, :], gate[:, None, :], out_grad, gate_pre, up_pre, w_gate, w_up, w_down,
        queries, keys, values, seg_row, seg_col, ends,
    )


def solution(mesh):
    row, col = P("ctx", None), P("ctx", "ep")
    both = ("ctx", "ep")
    pre, weight = P(both, None, None, None), P(both, None, None)
    return jax.shard_map(
        local,
        mesh=mesh,
        in_specs=(row, row, row, P("ctx"), pre, pre, weight, weight, weight, col, col, col),
        out_specs=(col, col, col, weight),
        check_vma=False,
    )
```

time: 284 us -> 186 us (0.65)
  the two profiles are of different devices: /device:TPU:1 before, /device:TPU:135 now
where the time goes in v2:
time: 186 us; the launch traced here: 185 us
  Pallas kernels  167 us (90%)
  local copies, waits for them, and re-layouts  15.1 us (8%)
  other arithmetic  2.33 us (1%)
    pallas_call x1, Pallas kernels, local(): pl.pallas_call(kernel, out_shape=(small, small, small, jax.ShapeDtypeStru...  167 us
    unnamed x4, local copies, waits for them, and re-layouts  7.84 us

profile of v2, /device:TPU:135, one launch (start us, length us, event | category | flops | bytes accessed | tf_op | source)
XLA Modules:
  0.0 185.4 jit_solution(13150826813584464983)
XLA Ops:
  0.7 1.3 fusion.11
  2.1 0.6 broadcast_in_dim.50
  2.7 0.7 concatenate.5
  3.4 0.7 concatenate.6.ends
  4.0 0.7 convert_bitcast_fusion
  4.7 0.8 compare_reduce_fusion
  5.5 1.3 broadcast_in_dim.48.seg_row
  6.8 0.8 fusion
  7.6 0.6 broadcast_in_dim.47.gate
  8.3 0.1 convolution_select_fusion
  8.4 0.6 broadcast_in_dim.44.rank
  9.1 1.4 broadcast_in_dim.49.seg_col
  10.5 167.1 %shard_map.147 = (bf16[256,256]{1,0:T(8,128)(2,1)}, bf16[256,256]{1,0:T(8,128)(2,1)}, bf16[256,256]{1,0:T(8,128)(2,1)}, f32[1,256,2048]{2,1,0:T(8,128)}) custom-call(f32[32,1,256]{2,1,0:T(1,128)} %broadcast_in_dim.44.rank, f32[32,1,256]{2,1,0:T(1,128)} %broadcast_in_dim.47.gate, bf16[256,2048]{1,0:T(8,128)(2,1)} %rows_in.1, ...), custom_call_target="tpu_custom_call" | custom-call | tf_op jit(solution)/shard_map/pallas_call | solution.py:338
  177.6 1.6 copy.20
  179.2 1.6 copy.21
  180.7 1.6 copy.22
  182.3 3.1 %copy.23 = f32[1,256,2048]{2,1,0:T(8,128)} copy(f32[1,256,2048]{2,1,0:T(8,128)} %get-tuple-element.13) | data formatting | bytes 4194304
  (1 shorter events, 0.0 us)

commit v3 on v2

v3 whole, which is shorter than its diff:
```python
import jax
import jax.numpy as jnp
from jax import lax
from jax.experimental import pallas as pl
from jax.experimental.pallas import tpu as pltpu
from jax.sharding import PartitionSpec as P

HEAD_DIM = 128
MESH = pl.DeviceIdType.MESH
BF16, F32, I32 = jnp.bfloat16, jnp.float32, jnp.int32
OWNERS, GROUPS = 32, 8
SLOTS, TOKENS, WIDTH, HIDDEN = 48, 256, 2048, 256
GIVE, PASS = 1536, 512
TAKE, SHARE = 1280, 768
SPAN = 256
LAID = (0, 4, 6, 2, 7, 1, 3, 5)
DIRECT, OWN = (TAKE - SHARE) // SPAN, SHARE // SPAN
STEP = 2
STEPS, ROWS = OWNERS // STEP, STEP * SLOTS
HOLD = 2
REACH = 7


def dot(a, b, dims):
    return lax.dot_general(a, b, (dims, ((), ())), preferred_element_type=F32)


def place(me):
    return me // 8, (me // 2) % 4, me % 2


def offset(slot):
    o = (13 * slot) % 32
    return o // 8, (o // 2) % 4, o % 2


def owner_vector(me, slots):
    (y, x, c), o = place(me), (13 * slots) & 31
    dy, dx, dc = o >> 3, (o >> 1) & 3, o & 1
    a, b = dy + c * (dx - dy), dx + c * (dy - dx)
    return ((y + a) & 3) * 8 + ((x + b) & 3) * 2 + ((c + dc) & 1)


def dest(me, slot):
    (y, x, c), (dy, dx, dc) = place(me), offset(slot)
    a, b = dy + c * (dx - dy), dx + c * (dy - dx)
    return ((y + a) % 4) * 8 + ((x + b) % 4) * 2 + (c + dc) % 2


def source(me, slot):
    (y, x, c), (dy, dx, dc) = place(me), offset(slot)
    s = (c + dc) % 2
    a, b = dy + s * (dx - dy), dx + s * (dy - dx)
    return ((y + 4 - a) % 4) * 8 + ((x + 4 - b) % 4) * 2 + s


def kernel(
    ids, gates, segment, rows_in, gate_pre, up_pre, w_gate, w_up, w_down, q_ref, k_ref, v_ref,
    small_out, down_out,
    rank, gate, ends, seg_col, send, cot, part, part_in, back, got, got_direct, hidden, y_sum, y_out, y_in, y_acc, state_out, state_in, ends_in, scores, carried,
    send_s, send_r, pass_s, pass_r, pair_s, pair_r, back_s, back_r, direct_s, direct_r, y_s, y_r, state_s, state_r, ends_s, ends_r,
):
    me, z = lax.axis_index("ctx"), lax.axis_index("ep")
    half = z % 2
    mate = z + 1 - 2 * half
    base = pl.multiple_of(half * (WIDTH - GIVE), 128)
    mine = pl.multiple_of(half * TAKE, 128)
    theirs = pl.multiple_of((1 - half) * TAKE, 128)

    def remote(src, dst, s, r, ctx, ep):
        return pltpu.make_async_remote_copy(src, dst, s, r, device_id=(ctx, ep), device_id_type=MESH)

    def sending(i):
        return remote(send.at[i], cot.at[i, :, pl.ds(base, GIVE)], send_s.at[i], send_r.at[i], dest(me, i), z)

    def passing(i):
        columns = cot.at[i, :, pl.ds(pl.multiple_of(half * GIVE, 128), PASS)]
        return remote(columns, columns, pass_s.at[i], pass_r.at[i], me, mate)

    def passed(i):
        columns = cot.at[i, :, pl.ds(pl.multiple_of((1 - half) * GIVE, 128), PASS)]
        return remote(columns, columns, pass_s.at[i], pass_r.at[i], me, mate)

    def pairing(i):
        return remote(part.at[i, :, pl.ds(theirs, SHARE)], part_in.at[i], pair_s.at[i], pair_r.at[i], me, mate)

    def returning(i):
        return remote(back.at[i], got.at[i], back_s.at[i], back_r.at[i], source(me, i), z)

    def directing(i):
        columns = part.at[i, :, pl.ds(SHARE, TAKE - SHARE)]
        return remote(columns, got_direct.at[i], direct_s.at[i], direct_r.at[i], source(me, i), z)

    def shard(j):
        return (me + 1 + j) % OWNERS if j < REACH else (me + OWNERS - (j - REACH + 1)) % OWNERS

    def telling(j):
        return remote(ends, ends_in.at[j], ends_s.at[j], ends_r.at[j], shard(j), z)

    def stating(j):
        return remote(state_out.at[j // REACH], state_in.at[j], state_s.at[j], state_r.at[j], shard(j), z)

    barrier = pltpu.get_barrier_semaphore()

    @pl.loop(1, OWNERS)
    def _(i):
        pl.semaphore_signal(barrier, 1, device_id=((me + i) % OWNERS, z), device_id_type=MESH)

    @pl.loop(1, GROUPS)
    def _(i):
        pl.semaphore_signal(barrier, 1, device_id=(me, (z + i) % GROUPS), device_id_type=MESH)

    rows_at = lax.broadcasted_iota(I32, (TOKENS, TOKENS), 0)
    cols_at = lax.broadcasted_iota(I32, (TOKENS, TOKENS), 1)
    experts_at = 2 * owner_vector(me, lax.broadcasted_iota(I32, (OWNERS, TOKENS), 0)) + z // (GROUPS // 2)
    named = jnp.zeros((OWNERS, TOKENS), F32)
    weight_of = jnp.zeros((OWNERS, TOKENS), F32)
    for k in range(ids.shape[0]):
        hit = ids[k : k + 1, :] == experts_at
        named = jnp.where(hit, 1.0, named)
        weight_of = jnp.where(hit, gates[k : k + 1, :].astype(F32), weight_of)
    before = dot(named.astype(BF16), jnp.where(rows_at < cols_at, 1.0, 0.0).astype(BF16), ((1,), (0,)))
    rank[...] = jnp.where(named > 0.0, before, -1.0)
    gate[...] = weight_of
    seg_row = segment[...].astype(F32)
    seg_col[...] = jnp.transpose(jnp.broadcast_to(seg_row, (128, TOKENS)))
    ends[0:8, :] = jnp.broadcast_to(seg_col[0:1, :], (8, 128))
    ends[8:16, :] = jnp.broadcast_to(seg_col[TOKENS - 1 : TOKENS, :], (8, 128))
    slot_of = lax.broadcasted_iota(I32, (SLOTS, TOKENS), 0).astype(F32)

    def seats(g, weighted):
        blocks = []
        for j in range(STEP):
            at = pl.ds(g * STEP + j, 1)
            seated = slot_of == rank[at, :]
            blocks.append(jnp.where(seated, gate[at, :] if weighted else 1.0, 0.0).astype(BF16))
        return jnp.concatenate(blocks, axis=0)

    def fill(g):
        made = dot(seats(g, True), rows_in[:, pl.ds(base, GIVE)], ((1,), (0,)))
        send[pl.ds(g * STEP, STEP)] = made.astype(BF16).reshape(STEP, SLOTS, GIVE)

    fill(0)
    pl.semaphore_wait(barrier, OWNERS + GROUPS - 2)

    for j in range(2 * REACH):
        telling(j).start()

    @pl.loop(0, STEPS)
    def _(g):
        @pl.when(g > 0)
        def _():
            fill(g)

        for j in range(STEP):

            @pl.when(g * STEP + j > 0)
            def _():
                sending(g * STEP + j).start()

    own = jnp.where(slot_of == rank[0:1, :], gate[0:1, :], 0.0).astype(BF16)
    cot[0] = dot(own, rows_in[...], ((1,), (0,))).astype(BF16)

    first_mask = seg_col[...] == ends[0:1, :]
    last_mask = seg_col[...] == ends[8:9, :]
    for h in range(2):
        head = slice(h * HEAD_DIM, (h + 1) * HEAD_DIM)
        held = jnp.where(last_mask, k_ref[:, head].astype(F32), 0.0).astype(BF16)
        state_out[0, h] = dot(held, v_ref[:, head], ((0,), (0,))).astype(BF16)
    for j in range(REACH):
        stating(j).start()

    def experts(g):
        these = pl.ds(g * STEP, STEP)
        rows = cot[these].reshape(ROWS, WIDTH)
        down_part = dot(rows, w_down[0], ((1,), (1,)))
        a = jnp.concatenate([gate_pre[0, source(me, g * STEP + j)] for j in range(STEP)], axis=0).astype(F32)
        u = jnp.concatenate([up_pre[0, source(me, g * STEP + j)] for j in range(STEP)], axis=0).astype(F32)
        s = jax.nn.sigmoid(a)
        hidden[pl.ds(g * ROWS, ROWS), :] = (a * s * u).astype(BF16)
        gate_delta = (down_part * u * s * (1.0 + a * (1.0 - s))).astype(BF16)
        up_delta = (down_part * a * s).astype(BF16)
        for n in (3, 4, 0, 1, 2, 5, 6, 7):
            columns = slice(LAID[n] * SPAN, (LAID[n] + 1) * SPAN)
            total = dot(gate_delta, w_gate[0, columns, :], ((1,), (1,)))
            total += dot(up_delta, w_up[0, columns, :], ((1,), (1,)))
            part[these, :, n * SPAN : (n + 1) * SPAN] = total.astype(BF16).reshape(STEP, SLOTS, SPAN)

    @pl.loop(0, STEPS + 2)
    def _(t):
        @pl.when(t < STEPS)
        def _():
            for j in range(STEP):

                @pl.when(t * STEP + j > 0)
                def _():
                    sending(t * STEP + j).wait_recv()
                    passing(t * STEP + j).start()

        @pl.when((t > 0) & (t < STEPS + 1))
        def _():
            g = t - 1
            for j in range(STEP):

                @pl.when(g * STEP + j > 0)
                def _():
                    passed(g * STEP + j).wait_recv()

            experts(g)
            for j in range(STEP):
                pairing(g * STEP + j).start()

                @pl.when(g * STEP + j > 0)
                def _():
                    directing(g * STEP + j).start()

        @pl.when(t > 1)
        def _():
            g = t - 2
            for j in range(STEP):
                pairing(g * STEP + j).wait_recv()
            these = pl.ds(g * STEP, STEP)
            summed = part[these, :, pl.ds(mine, SHARE)].astype(F32) + part_in[these].astype(F32)
            back[these] = summed.astype(BF16)

            @pl.when(t >= HOLD)
            def _():
                for j in range(STEP):

                    @pl.when(g * STEP + j > 0)
                    def _():
                        returning(g * STEP + j).start()

        @pl.when(t == HOLD)
        def _():
            @pl.loop(1, (HOLD - 2) * STEP)
            def _(i):
                returning(i).start()

    got[0] = back[0]
    got_direct[0] = part[0, :, SHARE:TAKE]

    allowed = (rows_at >= cols_at) & (jnp.concatenate([seg_col[...]] * 2, axis=1) == seg_row)

    def arrived(backward):
        total = jnp.zeros((2, HEAD_DIM, HEAD_DIM), F32)
        for j in range(REACH):
            k = backward * REACH + j
            stating(k).wait_recv()
            if backward:
                same = ends_in[k, 0:1, :] == ends[8:9, :]
                inside = jnp.where(me + 1 + j < OWNERS, 1.0, 0.0)
            else:
                same = ends_in[k, 8:9, :] == ends[0:1, :]
                inside = jnp.where(me - 1 - j >= 0, 1.0, 0.0)
            weight = jnp.where(same, 1.0, 0.0) * inside
            total += state_in[k].astype(F32) * weight[None]
        return total.astype(BF16)

    for j in range(2 * REACH):
        telling(j).wait_recv()
    carried[...] = arrived(0)
    for h in range(2):
        head = slice(h * HEAD_DIM, (h + 1) * HEAD_DIM)
        scores[h] = jnp.where(allowed, dot(q_ref[:, head], k_ref[:, head], ((1,), (1,))), 0.0).astype(BF16)

    y_acc[...] = jnp.zeros_like(y_acc)

    def spreading(b, to):
        return remote(y_out.at[b], y_in.at[z], y_s.at[b], y_r.at[z], me, to)

    def spread(i):
        return remote(y_out.at[0], y_in.at[i], y_s.at[0], y_r.at[i], me, z)

    def out_of(b, to):
        @pl.when(to != z)
        def _():
            spreading(b, to).start()

        @pl.when(to == z)
        def _():
            y_acc[...] = y_sum[:, b * SPAN : (b + 1) * SPAN]

    y_sum[...] = jnp.zeros_like(y_sum)

    @pl.loop(0, STEPS)
    def _(g):
        for j in range(STEP):

            @pl.when(g * STEP + j > 0)
            def _():
                directing(g * STEP + j).wait_recv()

        rows = got_direct[pl.ds(g * STEP, STEP)].reshape(ROWS, TAKE - SHARE)
        y_sum[:, 0 : TAKE - SHARE] += dot(seats(g, False), rows, ((0,), (0,)))

    for b in range(DIRECT):
        y_out[b] = y_sum[:, b * SPAN : (b + 1) * SPAN].astype(BF16)
        out_of(b, LAID[OWN + b])

    for n in range(WIDTH // 256):
        columns = slice(n * 256, (n + 1) * 256)
        down_out[0, :, columns] = dot(
            hidden[...], cot[:, :, columns].reshape(OWNERS * SLOTS, 256), ((0,), (0,))
        )

    @pl.loop(0, STEPS)
    def _(g):
        for j in range(STEP):

            @pl.when(g * STEP + j > 0)
            def _():
                returning(g * STEP + j).wait_recv()

        rows = got[pl.ds(g * STEP, STEP)].reshape(ROWS, SHARE)
        y_sum[:, TAKE - SHARE : TAKE] += dot(seats(g, False), rows, ((0,), (0,)))

    for b in range(OWN):
        y_out[DIRECT + b] = y_sum[:, (DIRECT + b) * SPAN : (DIRECT + b + 1) * SPAN].astype(BF16)
        even, odd = LAID[b], LAID[OWN + DIRECT + b]
        out_of(DIRECT + b, even + half * (odd - even))

    is_direct = (z == LAID[OWN]) | (z == LAID[OWN + 1])
    odd_own = (z == LAID[5]) | (z == LAID[6]) | (z == LAID[7])
    for i in range(GROUPS):
        wanted = is_direct | odd_own if i % 2 else jnp.logical_not(odd_own)

        @pl.when((z != i) & wanted)
        def _():
            spread(i).wait_recv()
            y_acc[...] += y_in[i].astype(F32)

    for h in range(2):
        head = slice(h * HEAD_DIM, (h + 1) * HEAD_DIM)
        opened = jnp.where(first_mask, q_ref[:, head].astype(F32), 0.0).astype(BF16)
        state_out[1, h] = dot(opened, y_acc[:, head].astype(BF16), ((0,), (0,))).astype(BF16)
    for j in range(REACH, 2 * REACH):
        stating(j).start()

    inner = []
    for h in range(2):
        head = slice(h * HEAD_DIM, (h + 1) * HEAD_DIM)
        g_h = y_acc[:, head].astype(BF16)
        cot_value = jnp.where(allowed, dot(g_h, v_ref[:, head], ((1,), (1,))), 0.0).astype(BF16)
        query_grad = dot(cot_value, k_ref[:, head], ((1,), (0,)))
        query_grad += jnp.where(first_mask, dot(g_h, carried[h], ((1,), (1,))), 0.0)
        small_out[0, :, head] = query_grad.astype(BF16)
        inner.append((dot(cot_value, q_ref[:, head], ((0,), (0,))), dot(scores[h], g_h, ((0,), (0,)))))

    back_state = arrived(1)
    for h in range(2):
        head = slice(h * HEAD_DIM, (h + 1) * HEAD_DIM)
        key_grad, value_grad = inner[h]
        key_part = dot(v_ref[:, head], back_state[h], ((1,), (1,)))
        value_part = dot(k_ref[:, head], back_state[h], ((1,), (0,)))
        small_out[1, :, head] = (key_grad + jnp.where(last_mask, key_part, 0.0)).astype(BF16)
        small_out[2, :, head] = (value_grad + jnp.where(last_mask, value_part, 0.0)).astype(BF16)

    pairing(0).wait_send()

    @pl.loop(1, OWNERS)
    def _(i):
        sending(i).wait_send()
        passing(i).wait_send()
        pairing(i).wait_send()
        returning(i).wait_send()
        directing(i).wait_send()

    for b in range(DIRECT + OWN):
        if b < DIRECT:
            to = LAID[OWN + b]
        else:
            to = LAID[b - DIRECT] + half * (LAID[OWN + b] - LAID[b - DIRECT])

        @pl.when(to != z)
        def _():
            spreading(b, to).wait_send()

    for j in range(2 * REACH):
        telling(j).wait_send()
        stating(j).wait_send()


def hand_over(grads, down_grad, q_out, k_out, v_out, down_out):
    for i, out in enumerate((q_out, k_out, v_out)):
        out[...] = grads[i]
    down_out[...] = down_grad[...]


def local(
    out_grad, gate_values, expert_ids, segment_ids, gate_pre, up_pre, w_gate, w_up, w_down, queries, keys, values
):
    vmem = pl.BlockSpec(memory_space=pltpu.VMEM)
    dma = pltpu.SemaphoreType.DMA
    small = jax.ShapeDtypeStruct((3, TOKENS, SPAN), BF16)
    down = jax.ShapeDtypeStruct((1, HIDDEN, WIDTH), F32)
    states = (2, HEAD_DIM, HEAD_DIM)
    grads, down_grad = pl.pallas_call(
        kernel,
        out_shape=(small, down),
        in_specs=[vmem] * 12,
        out_specs=(vmem,) * 2,
        scratch_shapes=[
            pltpu.VMEM((OWNERS, TOKENS), F32),
            pltpu.VMEM((OWNERS, TOKENS), F32),
            pltpu.VMEM((16, 128), F32),
            pltpu.VMEM((TOKENS, 128), F32),
            pltpu.VMEM((OWNERS, SLOTS, GIVE), BF16),
            pltpu.VMEM((OWNERS, SLOTS, WIDTH), BF16),
            pltpu.VMEM((OWNERS, SLOTS, WIDTH), BF16),
            pltpu.VMEM((OWNERS, SLOTS, SHARE), BF16),
            pltpu.VMEM((OWNERS, SLOTS, SHARE), BF16),
            pltpu.VMEM((OWNERS, SLOTS, SHARE), BF16),
            pltpu.VMEM((OWNERS, SLOTS, TAKE - SHARE), BF16),
            pltpu.VMEM((OWNERS * SLOTS, HIDDEN), BF16),
            pltpu.VMEM((TOKENS, TAKE), F32),
            pltpu.VMEM((DIRECT + OWN, TOKENS, SPAN), BF16),
            pltpu.VMEM((GROUPS, TOKENS, SPAN), BF16),
            pltpu.VMEM((TOKENS, SPAN), F32),
            pltpu.VMEM((2, *states), BF16),
            pltpu.VMEM((2 * REACH, *states), BF16),
            pltpu.VMEM((2 * REACH, 16, 128), F32),
            pltpu.VMEM((2, TOKENS, TOKENS), BF16),
            pltpu.VMEM(states, BF16),
            *[dma((OWNERS,))] * 10,
            dma((DIRECT + OWN,)), dma((GROUPS,)), *[dma((2 * REACH,))] * 4,
        ],
        compiler_params=pltpu.CompilerParams(
            collective_id=0, has_side_effects=True, vmem_limit_bytes=58 << 20
        ),
    )(
        expert_ids.T, gate_values.T, segment_ids[None, :], out_grad, gate_pre, up_pre, w_gate, w_up, w_down,
        queries, keys, values,
    )
    one = jax.ShapeDtypeStruct((TOKENS, SPAN), BF16)
    return pl.pallas_call(
        hand_over,
        out_shape=(one, one, one, down),
        in_specs=[vmem, vmem],
        out_specs=(vmem,) * 4,
        compiler_params=pltpu.CompilerParams(vmem_limit_bytes=8 << 20),
    )(grads, down_grad)


def solution(mesh):
    row, col = P("ctx", None), P("ctx", "ep")
    both = ("ctx", "ep")
    pre, weight = P(both, None, None, None), P(both, None, None)
    return jax.shard_map(
        local,
        mesh=mesh,
        in_specs=(row, row, row, P("ctx"), pre, pre, weight, weight, weight, col, col, col),
        out_specs=(col, col, col, weight),
        check_vma=False,
    )
```

time: 186 us -> 156 us (0.84)
  the two profiles are of different devices: /device:TPU:135 before, /device:TPU:1 now
where the time goes in v3:
time: 156 us; the launch traced here: 153 us
  Pallas kernels  150 us (96%)
  local copies, waits for them, and re-layouts  2.58 us (2%)
    pallas_call x1, Pallas kernels, local(): pl.pallas_call(kernel, out_shape=(small, down), in_specs=[vmem] * 12, out...  148 us

profile of v3, /device:TPU:1, one launch (start us, length us, event | category | flops | bytes accessed | tf_op | source)
XLA Modules:
  0.0 153.3 jit_solution(16214258499024362196)
XLA Ops:
  0.6 148.5 %shard_map.147 = (bf16[3,256,256]{2,1,0:T(8,128)(2,1)}, f32[1,256,2048]{2,1,0:T(8,128)}) custom-call(s32[8,256]{1,0:T(8,128)} %bitcast.3, bf16[8,256]{1,0:T(8,128)(2,1)} %bitcast.4, s32[1,256]{1,0:T(1,128)} %bitcast.5, bf16[256,2048]{1,0:T(8,128)(2,1)} %rows_in.1, bf16[1,32,48,256]{3,2,1,0:T(8,128)(2,1)} %gate_pre.1, bf16[1,32,48,256]{3,2,1,0:T(8,128)(2,1)} %up_pre.1, ...), custom_call_target="tpu_custom_call" | custom-call | tf_op jit(solution)/shard_map/pallas_call | solution.py:398
  149.1 0.0 copy-start
  149.1 1.6 %copy-done = f32[1,256,2048]{2,1,0:T(8,128)S(1)} copy-done((f32[1,256,2048]{2,1,0:T(8,128)S(1)}, f32[1,256,2048]{2,1,0:T(8,128)}, u32[]{:S(2)}) %copy-start) | copy-done | bytes 2097176
  150.7 0.0 copy-start.1
  150.7 1.0 copy-done.1
  151.7 1.6 %shard_map.148 = (bf16[256,256]{1,0:T(8,128)(2,1)}, bf16[256,256]{1,0:T(8,128)(2,1)}, bf16[256,256]{1,0:T(8,128)(2,1)}, f32[1,256,2048]{2,1,0:T(8,128)}) custom-call(bf16[3,256,256]{2,1,0:T(8,128)(2,1)S(1)} %copy-done.1, f32[1,256,2048]{2,1,0:T(8,128)S(1)} %copy-done), custom_call_target="tpu_custom_call" | custom-call | tf_op jit(solution)/shard_map/pallas_call | solution.py:436
Async XLA Ops:
  149.1 1.6 %copy-start = (f32[1,256,2048]{2,1,0:T(8,128)S(1)}, f32[1,256,2048]{2,1,0:T(8,128)}, u32[]{:S(2)}) copy-start(f32[1,256,2048]{2,1,0:T(8,128)} %get-tuple-element.7.down_grad) | copy-start | bytes 6291460
  150.7 1.0 copy-start.1

commit v4 on v3

--- a/solution.py
+++ b/solution.py
@@ -12,12 +12,12 @@
 SLOTS, TOKENS, WIDTH, HIDDEN = 48, 256, 2048, 256
 GIVE, PASS = 1536, 512
 TAKE, SHARE = 1280, 768
-SPAN = 256
+SPAN, PIECE = 256, 64
 LAID = (0, 4, 6, 2, 7, 1, 3, 5)
 DIRECT, OWN = (TAKE - SHARE) // SPAN, SHARE // SPAN
 STEP = 2
 STEPS, ROWS = OWNERS // STEP, STEP * SLOTS
-HOLD = 2
+LATER, LAST = 2, 4
 REACH = 7
 
 
@@ -57,7 +57,7 @@
 def kernel(
     ids, gates, segment, rows_in, gate_pre, up_pre, w_gate, w_up, w_down, q_ref, k_ref, v_ref,
     small_out, down_out,
-    rank, gate, ends, seg_col, send, cot, part, part_in, back, got, got_direct, hidden, y_sum, y_out, y_in, y_acc, state_out, state_in, ends_in, scores, carried,
+    down, down_s, rank, gate, ends, seg_col, send, cot, part, part_in, back, got, got_direct, hidden, y_sum, y_out, y_in, y_acc, state_out, state_in, ends_in, scores, carried,
     send_s, send_r, pass_s, pass_r, pair_s, pair_r, back_s, back_r, direct_s, direct_r, y_s, y_r, state_s, state_r, ends_s, ends_r,
 ):
     me, z = lax.axis_index("ctx"), lax.axis_index("ep")
@@ -186,7 +186,7 @@
             total += dot(up_delta, w_up[0, columns, :], ((1,), (1,)))
             part[these, :, n * SPAN : (n + 1) * SPAN] = total.astype(BF16).reshape(STEP, SLOTS, SPAN)
 
-    @pl.loop(0, STEPS + 2)
+    @pl.loop(0, STEPS + LAST)
     def _(t):
         @pl.when(t < STEPS)
         def _():
@@ -197,9 +197,9 @@
                     sending(t * STEP + j).wait_recv()
                     passing(t * STEP + j).start()
 
-        @pl.when((t > 0) & (t < STEPS + 1))
-        def _():
-            g = t - 1
+        @pl.when((t >= LATER) & (t < STEPS + LATER))
+        def _():
+            g = t - LATER
             for j in range(STEP):
 
                 @pl.when(g * STEP + j > 0)
@@ -214,28 +214,20 @@
                 def _():
                     directing(g * STEP + j).start()
 
-        @pl.when(t > 1)
-        def _():
-            g = t - 2
+        @pl.when(t >= LAST)
+        def _():
+            g = t - LAST
             for j in range(STEP):
                 pairing(g * STEP + j).wait_recv()
             these = pl.ds(g * STEP, STEP)
             summed = part[these, :, pl.ds(mine, SHARE)].astype(F32) + part_in[these].astype(F32)
             back[these] = summed.astype(BF16)
 
-            @pl.when(t >= HOLD)
-            def _():
-                for j in range(STEP):
-
-                    @pl.when(g * STEP + j > 0)
-                    def _():
-                        returning(g * STEP + j).start()
-
-        @pl.when(t == HOLD)
-        def _():
-            @pl.loop(1, (HOLD - 2) * STEP)
-            def _(i):
-                returning(i).start()
+            for j in range(STEP):
+
+                @pl.when(g * STEP + j > 0)
+                def _():
+                    returning(g * STEP + j).start()
 
     got[0] = back[0]
     got_direct[0] = part[0, :, SHARE:TAKE]
@@ -300,9 +292,11 @@
 
     for n in range(WIDTH // 256):
         columns = slice(n * 256, (n + 1) * 256)
-        down_out[0, :, columns] = dot(
+        down[:, columns] = dot(
             hidden[...], cot[:, :, columns].reshape(OWNERS * SLOTS, 256), ((0,), (0,))
         )
+    writing = pltpu.make_async_copy(down, down_out.at[0], down_s)
+    writing.start()
 
     @pl.loop(0, STEPS)
     def _(g):
@@ -356,6 +350,7 @@
         small_out[1, :, head] = (key_grad + jnp.where(last_mask, key_part, 0.0)).astype(BF16)
         small_out[2, :, head] = (value_grad + jnp.where(last_mask, value_part, 0.0)).astype(BF16)
 
+    writing.wait()
     pairing(0).wait_send()
 
     @pl.loop(1, OWNERS)
@@ -381,16 +376,26 @@
         stating(j).wait_send()
 
 
-def hand_over(grads, down_grad, q_out, k_out, v_out, down_out):
-    for i, out in enumerate((q_out, k_out, v_out)):
-        out[...] = grads[i]
-    down_out[...] = down_grad[...]
+def hand_over(grads, down_grad, q_out, k_out, v_out, down_out, small, large, come, go):
+    count = HIDDEN // PIECE
+    pieces = [pl.ds(i * PIECE, PIECE) for i in range(count)]
+    chain = [(down_grad.at[0, p], large.at[p], down_out.at[0, p]) for p in pieces]
+    chain += [(grads.at[i], small.at[i], out) for i, out in enumerate((q_out, k_out, v_out))]
+    into = [pltpu.make_async_copy(a, b, come.at[i]) for i, (a, b, _) in enumerate(chain)]
+    out_of = [pltpu.make_async_copy(b, c, go.at[i]) for i, (_, b, c) in enumerate(chain)]
+    for copy in into:
+        copy.start()
+    for first, then in zip(into, out_of):
+        first.wait()
+        then.start()
+    for copy in out_of:
+        copy.wait()
 
 
 def local(
     out_grad, gate_values, expert_ids, segment_ids, gate_pre, up_pre, w_gate, w_up, w_down, queries, keys, values
 ):
-    vmem = pl.BlockSpec(memory_space=pltpu.VMEM)
+    vmem, hbm = pl.BlockSpec(memory_space=pltpu.VMEM), pl.BlockSpec(memory_space=pl.ANY)
     dma = pltpu.SemaphoreType.DMA
     small = jax.ShapeDtypeStruct((3, TOKENS, SPAN), BF16)
     down = jax.ShapeDtypeStruct((1, HIDDEN, WIDTH), F32)
@@ -399,8 +404,10 @@
         kernel,
         out_shape=(small, down),
         in_specs=[vmem] * 12,
-        out_specs=(vmem,) * 2,
+        out_specs=(vmem, hbm),
         scratch_shapes=[
+            pltpu.VMEM((HIDDEN, WIDTH), F32),
+            dma,
             pltpu.VMEM((OWNERS, TOKENS), F32),
             pltpu.VMEM((OWNERS, TOKENS), F32),
             pltpu.VMEM((16, 128), F32),
@@ -436,9 +443,15 @@
     return pl.pallas_call(
         hand_over,
         out_shape=(one, one, one, down),
-        in_specs=[vmem, vmem],
-        out_specs=(vmem,) * 4,
-        compiler_params=pltpu.CompilerParams(vmem_limit_bytes=8 << 20),
+        in_specs=[hbm, hbm],
+        out_specs=(hbm,) * 4,
+        scratch_shapes=[
+            pltpu.VMEM((3, TOKENS, SPAN), BF16),
+            pltpu.VMEM((HIDDEN, WIDTH), F32),
+            dma((HIDDEN // PIECE + 3,)),
+            dma((HIDDEN // PIECE + 3,)),
+        ],
+        compiler_params=pltpu.CompilerParams(vmem_limit_bytes=60 << 20),
     )(grads, down_grad)
 
 

time: 156 us -> 152 us (0.974)
  local copies, waits for them, and re-layouts: 2.58 us -> 0 us
    unnamed x4 -> x0, local copies, waits for them, and re-layouts: 2.58 us -> none
    pallas_call x1, Pallas kernels: 148 us -> 147 us  [local(): pl.pallas_call(kernel, out_shape=(small, down), in_specs=[vmem] * 12, out...]
where the time goes in v4:
time: 152 us; the launch traced here: 150 us
  Pallas kernels  149 us (98%)
    pallas_call x1, Pallas kernels, local(): pl.pallas_call(kernel, out_shape=(small, down), in_specs=[vmem] * 12, out...  147 us

profile of v4, /device:TPU:1, one launch (start us, length us, event | category | flops | bytes accessed | tf_op | source)
XLA Modules:
  0.0 149.8 jit_solution(4478609795602446851)
XLA Ops:
  0.6 146.5 %shard_map.147 = (bf16[3,256,256]{2,1,0:T(8,128)(2,1)}, f32[1,256,2048]{2,1,0:T(8,128)}) custom-call(s32[8,256]{1,0:T(8,128)} %bitcast.3, bf16[8,256]{1,0:T(8,128)(2,1)} %bitcast.4, s32[1,256]{1,0:T(1,128)} %bitcast.5, bf16[256,2048]{1,0:T(8,128)(2,1)} %rows_in.1, bf16[1,32,48,256]{3,2,1,0:T(8,128)(2,1)} %gate_pre.1, bf16[1,32,48,256]{3,2,1,0:T(8,128)(2,1)} %up_pre.1, ...), custom_call_target="tpu_custom_call" | custom-call | tf_op jit(solution)/shard_map/pallas_call | solution.py:403
  147.2 2.6 %shard_map.148 = (bf16[256,256]{1,0:T(8,128)(2,1)}, bf16[256,256]{1,0:T(8,128)(2,1)}, bf16[256,256]{1,0:T(8,128)(2,1)}, f32[1,256,2048]{2,1,0:T(8,128)}) custom-call(bf16[3,256,256]{2,1,0:T(8,128)(2,1)} %get-tuple-element.6.grads, f32[1,256,2048]{2,1,0:T(8,128)} %get-tuple-element.7.down_grad), custom_call_target="tpu_custom_call" | custom-call | tf_op jit(solution)/shard_map/pallas_call | solution.py:443

commit v5 on v4

--- a/solution.py
+++ b/solution.py
@@ -81,8 +81,10 @@
         columns = cot.at[i, :, pl.ds(pl.multiple_of((1 - half) * GIVE, 128), PASS)]
         return remote(columns, columns, pass_s.at[i], pass_r.at[i], me, mate)
 
-    def pairing(i):
-        return remote(part.at[i, :, pl.ds(theirs, SHARE)], part_in.at[i], pair_s.at[i], pair_r.at[i], me, mate)
+    def pairing(g):
+        these = pl.ds(g * STEP, STEP)
+        columns = part.at[these, :, pl.ds(theirs, SHARE)]
+        return remote(columns, part_in.at[these], pair_s.at[g], pair_r.at[g], me, mate)
 
     def returning(i):
         return remote(back.at[i], got.at[i], back_s.at[i], back_r.at[i], source(me, i), z)
@@ -208,17 +210,16 @@
 
             experts(g)
             for j in range(STEP):
-                pairing(g * STEP + j).start()
 
                 @pl.when(g * STEP + j > 0)
                 def _():
                     directing(g * STEP + j).start()
+            pairing(g).start()
 
         @pl.when(t >= LAST)
         def _():
             g = t - LAST
-            for j in range(STEP):
-                pairing(g * STEP + j).wait_recv()
+            pairing(g).wait_recv()
             these = pl.ds(g * STEP, STEP)
             summed = part[these, :, pl.ds(mine, SHARE)].astype(F32) + part_in[these].astype(F32)
             back[these] = summed.astype(BF16)
@@ -351,13 +352,15 @@
         small_out[2, :, head] = (value_grad + jnp.where(last_mask, value_part, 0.0)).astype(BF16)
 
     writing.wait()
-    pairing(0).wait_send()
+
+    @pl.loop(0, STEPS)
+    def _(g):
+        pairing(g).wait_send()
 
     @pl.loop(1, OWNERS)
     def _(i):
         sending(i).wait_send()
         passing(i).wait_send()
-        pairing(i).wait_send()
         returning(i).wait_send()
         directing(i).wait_send()
 

time: 152 us -> 152 us (level)
  no operation moved by 1% of the time
where the time goes in v5:
time: 152 us; the launch traced here: 150 us
  Pallas kernels  149 us (98%)
    pallas_call x1, Pallas kernels, local(): pl.pallas_call(kernel, out_shape=(small, down), in_specs=[vmem] * 12, out...  147 us

profile of v5, /device:TPU:1, one launch (start us, length us, event | category | flops | bytes accessed | tf_op | source)
XLA Modules:
  0.0 149.8 jit_solution(14833667240382369374)
XLA Ops:
  0.6 146.6 %shard_map.147 = (bf16[3,256,256]{2,1,0:T(8,128)(2,1)}, f32[1,256,2048]{2,1,0:T(8,128)}) custom-call(s32[8,256]{1,0:T(8,128)} %bitcast.3, bf16[8,256]{1,0:T(8,128)(2,1)} %bitcast.4, s32[1,256]{1,0:T(1,128)} %bitcast.5, bf16[256,2048]{1,0:T(8,128)(2,1)} %rows_in.1, bf16[1,32,48,256]{3,2,1,0:T(8,128)(2,1)} %gate_pre.1, bf16[1,32,48,256]{3,2,1,0:T(8,128)(2,1)} %up_pre.1, ...), custom_call_target="tpu_custom_call" | custom-call | tf_op jit(solution)/shard_map/pallas_call | solution.py:406
  147.2 2.6 %shard_map.148 = (bf16[256,256]{1,0:T(8,128)(2,1)}, bf16[256,256]{1,0:T(8,128)(2,1)}, bf16[256,256]{1,0:T(8,128)(2,1)}, f32[1,256,2048]{2,1,0:T(8,128)}) custom-call(bf16[3,256,256]{2,1,0:T(8,128)(2,1)} %get-tuple-element.6.grads, f32[1,256,2048]{2,1,0:T(8,128)} %get-tuple-element.7.down_grad), custom_call_target="tpu_custom_call" | custom-call | tf_op jit(solution)/shard_map/pallas_call | solution.py:446
